TPU v7x, 512 devices: a whole 4x4x16 slice. The times are simulated.
512 devices in a mesh: dp: 16 (over z), ctx: 32 (over x, y, core).
Axes of the slice: x: 4, y: 4, z: 16, core: 2. Of those that a mesh axis runs over, the one named last changes fastest.
Arguments:
- queries: bfloat16 [16, 4096, 2048], P('dp', 'ctx'), may hold values from -4.5 to 4.5
- key_rows: bfloat16 [16, 4096, 2048], P('dp', 'ctx'), may hold values from -4.5 to 4.5
- value_rows: bfloat16 [16, 4096, 2048], P('dp', 'ctx'), may hold values from -6 to 6
- doc_ids: int32 [16, 4096], P('dp', 'ctx'), may hold values from 0 to 7, never falling along the last dimension, each value on 1 to 1024 neighbouring positions
- gate_logit: float32 [16], replicated, may hold values from -2 to 2
- grad_out: bfloat16 [16, 4096, 2048], P('dp', 'ctx'), may hold values from -6 to 6
Outputs:
- attended: bfloat16 [16, 4096, 2048], P('dp', 'ctx')
- grad_queries: bfloat16 [16, 4096, 2048], P('dp', 'ctx')
- grad_keys: bfloat16 [16, 4096, 2048], P('dp', 'ctx')
- grad_values: bfloat16 [16, 4096, 2048], P('dp', 'ctx')
- grad_gate: float32 [16], replicated
Inputs may be any that keep to these rules, and one draw needn't show every extreme that they name: `doc_ids`: within each stream ids start at 0, never fall and rise by one at each document start; all 8 documents occur, each of 1 to min(1024, 2048) tokens, one of exactly that many.
All inputs are finite; a program needn't handle non-finite values.
Results may differ from a plain program's by a relative error of at most 0.023.
Values may be sent and summed in bfloat16 or wider, within the bound.
A program may use at most 128 MiB of HBM per device.

v0:
```python
import jax
import jax.numpy as jnp
from jax import lax
from jax.sharding import PartitionSpec as P


def passed_along(value, axis, steps):
    count = lax.axis_size(axis)
    initial, last = (max(0, -steps), min(count, count - steps))
    return lax.ppermute(value, axis, [(source, source + steps) for source in range(initial, last)])


def carried_in(part, axis, combine, identity):
    place = lax.axis_index(axis)
    gathered = jax.tree.map(lambda a: lax.all_gather(a, axis), part)
    state = jax.tree.map(lambda a, e: jnp.zeros_like(a) + jnp.asarray(e, a.dtype), part, identity)

    def one(turn, state):
        return combine(
            state, jax.tree.map(lambda a: lax.dynamic_index_in_dim(a, turn, 0, False), gathered)
        )

    return lax.fori_loop(0, place, one, state)


def prefix(array, axis, combine, identity):
    count, place = (lax.axis_size(axis), lax.axis_index(axis))
    everything = jax.tree.map(
        lambda part, kind: lax.all_gather(part.astype(kind), axis),
        array,
        jax.tree.map(lambda a: jnp.bfloat16 if a.dtype == jnp.float32 else a.dtype, array),
    )
    start = jax.tree.map(
        lambda part, zero: jnp.broadcast_to(jnp.asarray(zero, part.dtype), part.shape),
        array,
        identity,
    )

    def turn(k, before):
        at = count - 1 - k
        reached = at > place
        new = combine(
            before, jax.tree.map(lambda part, own: part[at].astype(own.dtype), everything, array)
        )
        return jax.tree.map(lambda a, b: jnp.where(reached, a, b), new, before)

    return lax.fori_loop(0, count, turn, start)


def feature(inputs):
    return jax.nn.elu(inputs) + 1.0


def tail_state(key_feat, value_feat, weight):
    lifted = feature(key_feat) * weight[:, None, None]
    memory = jnp.einsum("shd,she->hde", lifted, value_feat, precision=lax.Precision.HIGHEST)
    return (memory, jnp.sum(lifted, axis=0))


def retrieve(query_feat, memory, key_total, use_memory):
    lifted = feature(query_feat) * use_memory[:, None, None]
    numerator = jnp.einsum("thd,hde->the", lifted, memory, precision=lax.Precision.HIGHEST)
    denominator = jnp.maximum(
        jnp.einsum("thd,hd->th", lifted, key_total, precision=lax.Precision.HIGHEST), 1.0
    )
    return numerator / denominator[:, :, None]


def attend(query_rows, key_block, value_block, allowed):
    scaling = query_rows.shape[-1] ** (-0.5)
    scores = (
        jnp.einsum("thd,shd->hts", query_rows, key_block, preferred_element_type=jnp.float32)
        * scaling
    )
    scores = jnp.where(allowed[None], scores, -jnp.inf)
    row_top = jnp.max(scores, axis=-1, keepdims=True)
    log_total = row_top + jnp.log(jnp.sum(jnp.exp(scores - row_top), axis=-1, keepdims=True))
    weights = jnp.exp(scores - log_total).astype(jnp.bfloat16)
    result = jnp.einsum("hts,shd->thd", weights, value_block, preferred_element_type=jnp.float32)
    return (result, log_total[..., 0])


def attend_back(query_rows, key_block, value_block, allowed, log_total, grad_att, row_delta):
    scaling = query_rows.shape[-1] ** (-0.5)
    scores = (
        jnp.einsum("thd,shd->hts", query_rows, key_block, preferred_element_type=jnp.float32)
        * scaling
    )
    scores = jnp.where(allowed[None], scores, -jnp.inf)
    softmax = jnp.exp(scores - log_total[..., None])
    weights = softmax.astype(jnp.bfloat16)
    grad_weights = jnp.einsum(
        "thd,shd->hts", grad_att, value_block, preferred_element_type=jnp.float32
    )
    grad_scores = (softmax * (grad_weights - row_delta[..., None]) * scaling).astype(jnp.bfloat16)
    grad_query = jnp.einsum(
        "hts,shd->thd", grad_scores, key_block, preferred_element_type=jnp.float32
    )
    grad_key = jnp.einsum(
        "hts,thd->shd", grad_scores, query_rows, preferred_element_type=jnp.float32
    )
    grad_value = jnp.einsum("hts,thd->shd", weights, grad_att, preferred_element_type=jnp.float32)
    return (grad_query, grad_key, grad_value)


def carry_combine(earlier, latter):
    keep = 1.0 - latter[2]
    return (
        latter[0] + keep[..., None, None] * earlier[0],
        latter[1] + keep[..., None] * earlier[1],
        jnp.maximum(earlier[2], latter[2]),
    )


def on_device(queries, key_rows, value_rows, doc_ids, gate_logit, grad_out):
    head_count = gate_logit.shape[0]
    seg_rows = queries.shape[1]
    row_width = queries.shape[2]
    block_shape = (seg_rows, head_count, row_width // head_count)
    gate = jax.nn.sigmoid(gate_logit)
    prior_keys, prior_values = passed_along((key_rows, value_rows), "ctx", 1)
    prior_ids = passed_along(doc_ids + 1, "ctx", 1) - 1
    own_ids = doc_ids[0]
    before_ids = prior_ids[0]
    query_blk = queries[0].reshape(block_shape)
    key_blk = key_rows[0].reshape(block_shape)
    value_blk = value_rows[0].reshape(block_shape)
    window_keys = jnp.concatenate([prior_keys[0].reshape(block_shape), key_blk], axis=0)
    window_values = jnp.concatenate([prior_values[0].reshape(block_shape), value_blk], axis=0)
    window_ids = jnp.concatenate([before_ids, own_ids])
    row_pos = jnp.arange(seg_rows)[:, None]
    col_pos = jnp.arange(2 * seg_rows)[None, :]
    allowed = (
        (col_pos > row_pos)
        & (col_pos <= row_pos + seg_rows)
        & (window_ids[None, :] == own_ids[:, None])
    )
    local_out, log_total = attend(query_blk, window_keys, window_values, allowed)
    last_prior = before_ids[-1]
    last_own = own_ids[-1]
    weight = (own_ids == last_own).astype(jnp.float32)
    resets = jnp.reshape(last_own != last_prior, (1,)).astype(jnp.float32)
    use_memory = (own_ids == last_prior).astype(jnp.float32)

    def own_tail(key_feat, value_feat):
        return tail_state(key_feat, value_feat, weight)

    (tail_mem, tail_total), tail_pull = jax.vjp(
        own_tail, key_blk.astype(jnp.float32), value_blk.astype(jnp.float32)
    )
    empty_state = (
        jnp.zeros_like(tail_mem),
        jnp.zeros_like(tail_total),
        jnp.zeros((1,), jnp.float32),
    )
    prefix_mem, prefix_total, prefix_flag = carried_in(
        (tail_mem, tail_total, resets), "ctx", carry_combine, empty_state
    )

    def read_memory(query_feat, memory, key_total):
        return retrieve(query_feat, memory, key_total, use_memory)

    memory_out, read_pull = jax.vjp(
        read_memory, query_blk.astype(jnp.float32), prefix_mem, prefix_total
    )
    gate_col = gate[:, None]
    mixed = gate_col * memory_out + (1.0 - gate_col) * local_out
    grad_mixed = grad_out[0].reshape(block_shape).astype(jnp.float32)
    grad_gate_local = (
        jnp.sum(grad_mixed * (memory_out - local_out), axis=(0, 2)) * gate * (1.0 - gate)
    )
    grad_gate = lax.psum(grad_gate_local, ("dp", "ctx"))
    grad_att = ((1.0 - gate_col) * grad_mixed).astype(jnp.bfloat16)
    row_delta = jnp.sum(grad_att.astype(jnp.float32) * local_out, axis=-1).T
    grad_query_local, grad_window_keys, grad_window_values = attend_back(
        query_blk, window_keys, window_values, allowed, log_total, grad_att, row_delta
    )
    from_next_keys, from_next_values = passed_along(
        (grad_window_keys[:seg_rows], grad_window_values[:seg_rows]), "ctx", -1
    )
    grad_query_mem, grad_prefix_mem, grad_prefix_total = read_pull(gate_col * grad_mixed)
    carried_mem, carried_total, carried_flag = prefix(
        (grad_prefix_mem, grad_prefix_total, resets), "ctx", carry_combine, empty_state
    )
    grad_key_mem, grad_value_mem = tail_pull((carried_mem, carried_total))
    out_shape = (1, seg_rows, row_width)
    attended = mixed.astype(jnp.bfloat16).reshape(out_shape)
    grad_queries = (grad_query_local + grad_query_mem).astype(jnp.bfloat16).reshape(out_shape)
    grad_keys = (
        (grad_window_keys[seg_rows:] + from_next_keys + grad_key_mem)
        .astype(jnp.bfloat16)
        .reshape(out_shape)
    )
    grad_values = (
        (grad_window_values[seg_rows:] + from_next_values + grad_value_mem)
        .astype(jnp.bfloat16)
        .reshape(out_shape)
    )
    return (attended, grad_queries, grad_keys, grad_values, grad_gate)


def solution(mesh):
    placed = (
        P("dp", "ctx", None),
        P("dp", "ctx", None),
        P("dp", "ctx", None),
        P("dp", "ctx"),
        P(),
        P("dp", "ctx", None),
    )
    return jax.shard_map(
        on_device,
        mesh=mesh,
        in_specs=placed,
        out_specs=(
            P("dp", "ctx", None),
            P("dp", "ctx", None),
            P("dp", "ctx", None),
            P("dp", "ctx", None),
            P(),
        ),
        check_vma=False,
    )
```

profile of v0, /device:TPU:1, one launch (start us, length us, event | category | flops | bytes accessed | tf_op | source)
XLA Modules:
  0.0 629.7 jit_solution(9690049031526230840)
XLA Ops:
  7.9 4.6 collective-permute-start
  18.6 2.5 fusion.36
  29.1 67.0 %all-reduce = f32[32]{0:T(128)S(1)} all-reduce(f32[32]{0:T(128)S(1)} %dynamic-update-slice), channel_id=1, replica_groups=mesh['dp'=16,'ctx'=32] {'ctx'}, use_global_device_ids=true, to_apply=%add | all-reduce | flops 32 | bytes 256
  96.6 23.3 %all_gather.41 = f32[32,16,128]{2,1,0:T(8,128)S(1)} all-gather(f32[1,16,128]{2,1,0:T(8,128)S(1)} %bitcast.143), channel_id=1, replica_groups=mesh['dp'=16,'ctx'=32] {'ctx'}, dimensions={0}, use_global_device_ids=true | all-gather | bytes 270336 | tf_op jit(solution)/shard_map/all_gather | solution.py:15
  123.8 31.5 %all-gather.6.cloned.1.call-done = f32[512,128,128]{2,1,0:T(8,128)} async-done(((f32[16,128,128]{2,1,0:T(8,128)}), f32[512,128,128]{2,1,0:T(8,128)}) %all-gather.6.cloned.1.call-update) | async-done | bytes 33554448 | tf_op jit(solution)/shard_map/all_gather | solution.py:15
  155.5 3.4 while.32
  160.3 3.2 convolution_convert_fusion
  163.5 5.7 collective-permute-start.1
  170.0 158.9 %all-reduce.1 = bf16[32]{0:T(256)(128)(2,1)S(1)} all-reduce(bf16[32]{0:T(256)(128)(2,1)S(1)} %dynamic-update-slice.1), channel_id=1, replica_groups=mesh['dp'=16,'ctx'=32] {'ctx'}, use_global_device_ids=true, to_apply=%add.1 | all-reduce | flops 32 | bytes 128
  333.3 3.1 multiply_reduce_fusion
  339.2 6.6 %collective-permute-start.4 = (f32[128,16,128]{0,2,1:T(8,128)}, f32[128,16,128]{0,2,1:T(8,128)}, u32[]{:S(2)}, u32[]{:S(2)}) collective-permute-start(f32[128,16,128]{0,2,1:T(8,128)} %slice.29), channel_id=1, source_target_pairs={{1,0},{2,1},{3,2},{4,3},{5,4},{6,5},{7,6},{8,7},{9,8},{10,9},{11,1... | collective-permute-start | bytes 3145736 | tf_op jit(solution)/shard_map/ppermute | solution.py:10
  351.5 115.1 %psum.7 = f32[16]{0:T(128)} all-reduce(f32[16]{0:T(128)S(1)} %multiply_multiply_fusion), channel_id=1, replica_groups=mesh['dp'=16,'ctx'=32] {'dp','ctx'}, use_global_device_ids=true, to_apply=%region_10.11 | all-reduce | flops 16 | bytes 128 | tf_op jit(solution)/shard_map/psum | solution.py:172
  472.9 23.6 %all-gather.2 = bf16[512,128]{1,0:T(8,128)(2,1)S(1)} all-gather(bf16[16,128]{1,0:T(8,128)(2,1)S(1)} %convert_element_type.122), channel_id=4, replica_groups=mesh['dp'=16,'ctx'=32] {'ctx'}, dimensions={0}, use_global_device_ids=true | all-gather | bytes 135168 | tf_op jit(solution)/shard_map/all_gather | solution.py:29
  496.5 115.8 %while.33 = (s32[]{:T(128)}, f32[16,128,128]{2,1,0:T(8,128)S(1)}, f32[16,128]{1,0:T(8,128)S(1)}, s32[]{:T(128)}, bf16[32,16,128,128]{3,2,1,0:T(8,128)(2,1)}, /*i...) while((s32[]{:T(128)}, f32[16,128,128]{2,1,0:T(8,128)S(1)}, ...), condition=%wide.region_8.9_spmd.clone, body=%wide.region_7.8_spmd.clone.sunk | while | flops 1320969 | bytes 2642123 | solution.py:47
  497.1 2.4 fusion.108
  500.8 2.3 fusion.108
  504.4 2.3 fusion.108
  508.0 2.3 fusion.108
  511.6 2.3 fusion.108
  515.3 2.3 fusion.108
  518.9 2.3 fusion.108
  522.5 2.3 fusion.108
  526.1 2.3 fusion.108
  529.7 2.3 fusion.108
  533.3 2.3 fusion.108
  537.0 2.3 fusion.108
  544.2 2.3 fusion.108
  551.4 2.3 fusion.108
  569.5 2.3 fusion.108
  594.8 2.3 fusion.108
  612.3 4.5 fusion.30
  618.8 3.0 fusion.20
  (186 shorter events, 122.7 us)
Async XLA Ops:
  7.2 10.1 %copy-start.20 = (s32[1,128]{1,0:T(1,128)S(1)}, s32[1,128]{1,0:T(1,128)}, u32[]{:S(2)}) copy-start(s32[1,128]{1,0:T(1,128)} %param.13) | copy-start | bytes 1540
  7.2 148.2 %all-gather.6.cloned.1.call-start = ((), (), s32[]{:S(2)}) async-start(), calls=%async_computation | async-start | bytes 34603008 | tf_op jit(solution)/shard_map/all_gather | solution.py:15
  7.9 8.8 %collective-permute-start = (s32[1,128]{1,0:T(1,128)S(1)}, s32[1,128]{1,0:T(1,128)S(1)}, u32[]{:S(2)}, u32[]{:S(2)}) collective-permute-start(s32[1,128]{1,0:T(1,128)S(1)} %broadcast_add_fusion.1), channel_id=1, source_target_pairs={{0,1},{1,2},{2,3},{3,4},{4,5},{5,6},{6,7},{7,8},{8,9},{9,10},{10,1... | collective-permute-start | bytes 1544 | tf_op jit(solution)/shard_map/ppermute | solution.py:10
  15.0 8.2 %copy-start.5 = (bf16[1,128,2048]{1,2,0:T(8,128)(2,1)}, bf16[1,128,2048]{1,2,0:T(8,128)(2,1)S(1)}, u32[]{:S(2)}) copy-start(bf16[1,128,2048]{1,2,0:T(8,128)(2,1)S(1)} %copy.62) | copy-start | bytes 1572868
  16.5 329.3 %copy-start.8 = (bf16[1,128,2048]{1,2,0:T(8,128)(2,1)}, bf16[1,128,2048]{1,2,0:T(8,128)(2,1)S(1)}, u32[]{:S(2)}) copy-start(bf16[1,128,2048]{1,2,0:T(8,128)(2,1)S(1)} %copy.63) | copy-start | bytes 1572868
  18.6 5.7 copy-start.14
  21.1 3.5 copy-start.13
  21.1 5.9 copy-start.21
  21.1 74.9 %copy-start.10 = (bf16[1,128,2048]{2,1,0:T(8,128)(2,1)S(1)}, bf16[1,128,2048]{2,1,0:T(8,128)(2,1)}, u32[]{:S(2)}) copy-start(bf16[1,128,2048]{2,1,0:T(8,128)(2,1)} %param.11) | copy-start | bytes 1572868
  21.1 475.4 %all-gather.8.cloned.1.call-start = ((), (), s32[]{:S(2)}) async-start(), calls=%async_computation.1 | async-start | bytes 17301504 | tf_op jit(solution)/shard_map/all_gather | solution.py:29
  21.2 98.9 %collective-permute-start.2 = (bf16[1,128,2048]{1,2,0:T(8,128)(2,1)S(1)}, bf16[1,128,2048]{1,2,0:T(8,128)(2,1)}, u32[]{:S(2)}, u32[]{:S(2)}) collective-permute-start(bf16[1,128,2048]{1,2,0:T(8,128)(2,1)S(1)} %copy.62), channel_id=1, source_target_pairs={{0,1},{1,2},{2,3},{3,4},{4,5},{5,6},{6,7},{7,8},{8,9},{9,10},{10,1... | collective-permute-start | bytes 1572872 | tf_op jit(solution)/shard_map/ppermute | solution.py:10
  24.6 96.9 %copy-start.15 = (bf16[128,16,128]{2,0,1:T(8,128)(2,1)S(1)}, bf16[128,16,128]{2,0,1:T(8,128)(2,1)}, u32[]{:S(2)}) copy-start(bf16[128,16,128]{2,0,1:T(8,128)(2,1)} %copy.71) | copy-start | bytes 1572868
  121.4 0.8 copy-start.17
  122.2 1.3 copy-start
  158.9 1.4 copy-start.11
  163.5 165.4 %collective-permute-start.1 = (bf16[1,128,2048]{2,1,0:T(8,128)(2,1)}, bf16[1,128,2048]{2,1,0:T(8,128)(2,1)}, u32[]{:S(2)}, u32[]{:S(2)}) collective-permute-start(bf16[1,128,2048]{2,1,0:T(8,128)(2,1)} %param.12), channel_id=1, source_target_pairs={{0,1},{1,2},{2,3},{3,4},{4,5},{5,6},{6,7},{7,8},{8,9},{9,10},{10,1... | collective-permute-start | bytes 1572872 | tf_op jit(solution)/shard_map/ppermute | solution.py:10
  330.9 2.3 copy-start.1
  330.9 2.3 copy-start.9
  336.8 1.3 copy-start.2
  339.2 273.1 %collective-permute-start.4 = (f32[128,16,128]{0,2,1:T(8,128)}, f32[128,16,128]{0,2,1:T(8,128)}, u32[]{:S(2)}, u32[]{:S(2)}) collective-permute-start(f32[128,16,128]{0,2,1:T(8,128)} %slice.29), channel_id=1, source_target_pairs={{1,0},{2,1},{3,2},{4,3},{5,4},{6,5},{7,6},{8,7},{9,8},{10,9},{11,1... | collective-permute-start | bytes 3145736 | tf_op jit(solution)/shard_map/ppermute | solution.py:10
  346.7 2.9 copy-start.6
  347.1 1.3 copy-start.4
  349.6 269.3 %collective-permute-start.3 = (f32[128,16,128]{0,2,1:T(8,128)}, f32[128,16,128]{0,2,1:T(8,128)}, u32[]{:S(2)}, u32[]{:S(2)}) collective-permute-start(f32[128,16,128]{0,2,1:T(8,128)} %slice.27), channel_id=1, source_target_pairs={{1,0},{2,1},{3,2},{4,3},{5,4},{6,5},{7,6},{8,7},{9,8},{10,9},{11,1... | collective-permute-start | bytes 3145736 | tf_op jit(solution)/shard_map/ppermute | solution.py:10
  466.5 2.0 copy-start.12
  468.6 1.4 copy-start.7
  468.6 1.4 copy-start.16
  468.6 1.5 copy-start.18
  470.1 1.7 copy-start.19
  496.5 115.8 %copy-start.3 = (f32[256,16,128]{0,2,1:T(8,128)S(1)}, f32[256,16,128]{0,2,1:T(8,128)}, u32[]{:S(2)}) copy-start(f32[256,16,128]{0,2,1:T(8,128)} %copy-done.2) | copy-start | bytes 6291460
Sparse Core Ops, SparseCore 0:
  21.2 134.0 all-gather.5
  163.6 194.1 all-gather.7
where the time goes:
time: 634 us; the launch traced here: 630 us
  blocking collectives  388 us (61%)
  other arithmetic  121 us (19%)
  waiting for transfers between devices  31.7 us (5%)
  matrix products  26.1 us (4%)
  local copies, waits for them, and re-layouts  25.1 us (4%)
  starting transfers between devices  20.9 us (3%)
  between operations  15.8 us (2%)
    unnamed x2, blocking collectives  226 us
    psum x1, blocking collectives, on_device(): grad_gate = lax.psum(grad_gate_local, ('dp', 'ctx'))  115 us
    select_n x64, other arithmetic, turn(): return jax.tree.map(lambda a, b: jnp.where(reached, a, b), new, before)  96 us
    all_gather x1, waiting for transfers between devices, carried_in(): gathered = jax.tree.map(lambda a: lax.all_gather(a, axis), part)  31.5 us
    all_gather x1, blocking collectives, prefix(): lax.all_gather(part.astype(kind), axis)  23.6 us
    all_gather x1, blocking collectives, carried_in(): gathered = jax.tree.map(lambda a: lax.all_gather(a, axis), part)  23.3 us
    ppermute x5, starting transfers between devices, passed_along(): lax.ppermute(value, axis, [(source, source + steps) for source in range(i...  20.8 us
    sub x33, other arithmetic, carry_combine(): keep = 1.0 - latter[2]  19.3 us
  transfers between devices with their start and end apart: 7, of which 2 were waited for; matrix products, arithmetic and copies ran while one was open for 24% of the time, Pallas kernels for 0%

commit v1 on v0

v1 whole, which is shorter than its diff:
```python
import functools
import math

import jax
import jax.numpy as jnp
from jax import lax
from jax.experimental import pallas as pl
from jax.experimental.pallas import tpu as pltpu
from jax.sharding import PartitionSpec as P

SEG = 128
DIM = 128
HEADS = 16
ROW = 8
REACH = 8
MESH = pl.DeviceIdType.MESH
F32 = jnp.float32
BF16 = jnp.bfloat16


def dot_nn(a, b):
    return lax.dot_general(a, b, (((1,), (0,)), ((), ())), preferred_element_type=F32)


def dot_nt(a, b):
    return lax.dot_general(a, b, (((1,), (1,)), ((), ())), preferred_element_type=F32)


def dot_tn(a, b):
    return lax.dot_general(a, b, (((0,), (0,)), ((), ())), preferred_element_type=F32)


def place_of(h):
    return lax.rem(lax.div(h, 2), 2) * 8 + lax.div(h, 4) * 2 + lax.rem(h, 2)


def columns(h):
    return pl.ds(pl.multiple_of(h * DIM, DIM), DIM)


def feature(x):
    return jnp.where(x > 0, x + 1.0, jnp.exp(jnp.minimum(x, 0.0)))


def kernel(
    n_ctx, n_dp,
    q_in, k_in, v_in, ids_in, gate_in, g_in,
    att_out, dq_out, dk_out, dv_out, gg_out,
    q_s, k_s, v_s, g_s, idr, kp, vp, fk, fq, den_s,
    fx, fxp, ftc, fta, fro, fri, fpo, fpc, fsx, fres,
    bx, bxp, btc, bta, bro, bri, bpo, bpc, bsx, bres,
    ol, dql, dkl, dvl, dks, dvs, dkn, dvn,
    att_o, dq_o, dk_o, dv_o,
    zt, zr, zb, dzt, dzr, cz, gt, gg, bias, wm, um,
    red_s, red_r,
    load_sem, out_sem, ids_ss, ids_rs, z_ss, z_rs, dz_ss, dz_rs,
    k_ss, k_rs, v_ss, v_rs, dk_ss, dk_rs, dv_ss, dv_rs,
    f_ss, f_rs, b_ss, b_rs, red_ss, red_rs,
):
    me = lax.axis_index("ctx")
    mz = lax.axis_index("dp")
    row = lax.div(me, ROW)
    spot = lax.rem(me, ROW)
    y = lax.div(spot, 2)
    core = lax.rem(me, 2)

    def at(offset):
        return {"ctx": lax.rem(me + offset + n_ctx, n_ctx)}

    def up(offset):
        return {"dp": lax.rem(mz + offset + n_dp, n_dp)}

    def remote(src, dst, ss, rs, device):
        return pltpu.make_async_remote_copy(
            src_ref=src, dst_ref=dst, send_sem=ss, recv_sem=rs,
            device_id=device, device_id_type=MESH,
        )

    loads = []
    for i, (src, dst) in enumerate(
        ((ids_in, idr.at[REACH]), (k_in, k_s), (v_in, v_s), (q_in, q_s), (g_in, g_s))
    ):
        copy = pltpu.make_async_copy(src, dst, load_sem.at[i])
        copy.start()
        loads.append(copy)
    barrier = pltpu.get_barrier_semaphore()
    near = [d for d in range(-REACH, REACH + 1) if d] + [n_ctx // 2]
    steps_z = []
    d = 1
    while d < n_dp:
        steps_z.append(d)
        d *= 2
    far = sorted({s % n_dp for d in steps_z for s in (d, -d)})
    for d in near:
        pl.semaphore_signal(barrier, inc=1, device_id=at(d), device_id_type=MESH)
    for d in far:
        pl.semaphore_signal(barrier, inc=1, device_id=up(d), device_id_type=MESH)

    for h in range(HEADS):
        logit = jnp.full((1, DIM), gate_in[0, h], F32)
        gt[h] = 1.0 / (1.0 + jnp.exp(-logit))
    loads[0].wait()
    own_ids = idr[REACH]
    own_cols = jnp.broadcast_to(own_ids.astype(F32), (SEG, SEG))
    own_rows = jnp.transpose(own_cols)
    own_last = own_ids[:, SEG - 1 :].astype(F32)
    wm[...] = (own_rows == own_last).astype(F32)
    loads[1].wait()
    loads[2].wait()
    pl.semaphore_wait(barrier, len(near) + len(far))

    id_sends = [d for d in range(-(REACH - 1), REACH + 1) if d]
    for i, d in enumerate(id_sends):
        remote(idr.at[REACH], idr.at[REACH - d], ids_ss.at[i], ids_rs.at[i], at(d)).start()

    def send_kv(h, carry):
        remote(k_s.at[:, columns(h)], kp.at[h], k_ss.at[h], k_rs.at[h], at(1)).start()
        remote(v_s.at[:, columns(h)], vp.at[h], v_ss.at[h], v_rs.at[h], at(1)).start()
        return carry

    lax.fori_loop(0, HEADS, send_kv, 0)

    def tails(h, carry):
        lifted = feature(k_s[:, columns(h)].astype(F32)) * wm[...]
        short = lifted.astype(BF16)
        fk[h] = short
        zt[h] = jnp.sum(lifted, axis=0, keepdims=True)
        fx[place_of(h)] = dot_tn(short, v_s[:, columns(h)]).astype(BF16)
        return carry

    lax.fori_loop(0, HEADS, tails, 0, unroll=2)

    def pair_send(x, xp, ss, rs):
        other = pl.ds(pl.multiple_of((1 - core) * 8, 8), 8)
        return remote(x.at[other], xp, ss.at[0], rs.at[0], at(1 - 2 * core))

    f_pair = pair_send(fx, fxp, f_ss, f_rs)
    f_pair.start()
    for d in range(1, REACH + 1):
        remote(zt, zr.at[d - 1], z_ss.at[d - 1], z_rs.at[d - 1], at(d)).start()

    for i, d in enumerate(id_sends):
        remote(idr.at[REACH], idr.at[REACH - d], ids_ss.at[i], ids_rs.at[i], at(d)).wait()

    def last(offset):
        return idr[REACH + offset][:, SEG - 1 :]

    def same(a, b):
        return (last(a) == last(b)).astype(F32)

    is_late = core.astype(F32)
    is_early = 1.0 - is_late
    not_first = (me > 0).astype(F32)
    first_chip = (row > 0).astype(F32)
    last_row = (row < n_ctx // ROW - 1).astype(F32)
    early, late, before = -core, 1 - core, -1 - core
    m_in = same(early, late)
    m_before = same(early, before) * (me - core > 0).astype(F32)
    kappa = []
    for c in range(4):
        value = same(2 * c + 1 - spot, 2 * c - 1 - spot)
        kappa.append(value * first_chip if c == 0 else value)

    prev_ids = idr[REACH - 1]
    prev_rows = jnp.transpose(jnp.broadcast_to(prev_ids.astype(F32), (SEG, SEG)))
    s_pos = lax.broadcasted_iota(jnp.int32, (SEG, SEG), 0)
    t_pos = lax.broadcasted_iota(jnp.int32, (SEG, SEG), 1)
    cut = jnp.full((SEG, SEG), -1e30, F32)
    open_ = jnp.zeros((SEG, SEG), F32)
    shut = (1.0 - not_first) * -1e30
    bias[0] = jnp.where((s_pos > t_pos) & (prev_rows == own_cols), open_, cut) + shut
    bias[1] = jnp.where((s_pos <= t_pos) & (own_rows == own_cols), open_, cut)
    um[...] = (own_rows == prev_ids[:, SEG - 1 :].astype(F32)).astype(F32) * not_first

    def combine(x, xp, tc, ta, ss, rs, c_own, c_other):
        base = core * 8
        for i in range(8):
            tc[i] = (x[base + i].astype(F32) * c_own + xp[i].astype(F32) * c_other).astype(BF16)
        for i in range(2):
            ta[2 * y + i] = tc[2 * y + i]
        for dy in range(1, 4):
            a2a(tc, ta, ss, rs, 1, dy, True).start()

    def a2a(src, dst, ss, rs, slot, dy, sending):
        to_y = lax.rem(y + dy, 4)
        from_y = y if sending else lax.rem(y - dy + 4, 4)
        index = slot + dy - 1
        return remote(
            src.at[pl.ds(2 * to_y, 2)], dst.at[pl.ds(2 * from_y, 2)],
            ss.at[index], rs.at[index], {"ctx": row * ROW + 2 * to_y + core},
        )

    def ring_out(ta, ro, ri, tc, ss, rs, forward):
        for dy in range(1, 4):
            a2a(tc, ta, ss, rs, 1, dy, False).wait_recv()
        for i in range(2):
            total = None
            for c in range(4) if forward else range(3, -1, -1):
                block = ta[2 * c + i].astype(F32)
                total = block if total is None else block + kappa[c] * total
            ro[i] = total.astype(BF16)
        remote(ro, ri, ss.at[4], rs.at[4], at(ROW if forward else -ROW)).start()

    def spread(ta, ro, ri, po, pc, ss, rs, forward):
        remote(ro, ri, ss.at[4], rs.at[4], at(ROW if forward else -ROW)).wait_recv()
        gate_in_row = first_chip if forward else last_row
        for i in range(2):
            state = ri[i].astype(F32) * gate_in_row
            for c in range(4) if forward else range(3, -1, -1):
                po[2 * c + i] = state.astype(BF16)
                state = ta[2 * c + i].astype(F32) + kappa[c] * state
        for i in range(2):
            pc[2 * y + i] = po[2 * y + i]
        for dy in range(1, 4):
            a2a(po, pc, ss, rs, 5, dy, True).start()

    def finish_start(x, xp, po, pc, sx, res, ss, rs, r_other, r_state, s_own, s_state):
        for dy in range(1, 4):
            a2a(po, pc, ss, rs, 5, dy, False).wait_recv()
        base = core * 8
        for i in range(8):
            state = pc[i].astype(F32)
            sx[i] = (x[base + i].astype(F32) * s_own + state * s_state).astype(BF16)
        final(sx, res, ss, rs).start()
        for i in range(8):
            state = pc[i].astype(F32)
            res[base + i] = (xp[i].astype(F32) * r_other + state * r_state).astype(BF16)

    def final(sx, res, ss, rs, sending=True):
        base = pl.multiple_of((core if sending else 1 - core) * 8, 8)
        return remote(sx, res.at[pl.ds(base, 8)], ss.at[8], rs.at[8], at(1 - 2 * core))

    f_pair.wait_recv()
    combine(fx, fxp, ftc, fta, f_ss, f_rs, is_late + is_early * m_in, is_early + is_late * m_in)

    for d in range(1, REACH + 1):
        remote(zt, zr.at[d - 1], z_ss.at[d - 1], z_rs.at[d - 1], at(d)).wait_recv()
    total = jnp.zeros((HEADS, 1, DIM), F32)
    for d in range(1, REACH + 1):
        weight = same(-d, -1) * (me >= d).astype(F32)
        total = total + zr[d - 1] * weight
    zb[...] = total
    loads[3].wait()
    loads[4].wait()

    def state_part(h, carry):
        lifted = (feature(q_s[:, columns(h)].astype(F32)) * um[...]).astype(BF16)
        fq[h] = lifted
        totals = jnp.broadcast_to(zb[h], (DIM, DIM)).astype(BF16)
        den = dot_nt(lifted, totals)
        den_s[h] = den
        scaled = g_s[:, columns(h)].astype(F32) * gt[h] / jnp.maximum(den, 1.0)
        bx[place_of(h)] = dot_tn(lifted, scaled.astype(BF16)).astype(BF16)
        return carry

    lax.fori_loop(0, HEADS, state_part, 0, unroll=2)
    b_pair = pair_send(bx, bxp, b_ss, b_rs)
    b_pair.start()

    scaling = DIM ** -0.5
    scale2 = scaling * math.log2(math.e)

    def local(h, carry):
        remote(k_s.at[:, columns(h)], kp.at[h], k_ss.at[h], k_rs.at[h], at(1)).wait_recv()
        remote(v_s.at[:, columns(h)], vp.at[h], v_ss.at[h], v_rs.at[h], at(1)).wait_recv()
        q = q_s[:, columns(h)]
        k = k_s[:, columns(h)]
        v = v_s[:, columns(h)]
        keys, values = kp[h], vp[h]
        ga = (g_s[:, columns(h)].astype(F32) * (1.0 - gt[h])).astype(BF16)
        s0 = dot_nt(keys, q) * scale2 + bias[0]
        s1 = dot_nt(k, q) * scale2 + bias[1]
        top = jnp.max(jnp.maximum(s0, s1), axis=0, keepdims=True)
        e0 = jnp.exp2(s0 - top)
        e1 = jnp.exp2(s1 - top)
        inverse = 1.0 / jnp.sum(e0 + e1, axis=0, keepdims=True)
        w0 = e0 * inverse
        w1 = e1 * inverse
        gw0 = dot_nt(values, ga)
        gw1 = dot_nt(v, ga)
        delta = jnp.sum(w0 * gw0 + w1 * gw1, axis=0, keepdims=True)
        ds0 = (w0 * (gw0 - delta) * scaling).astype(BF16)
        ds1 = (w1 * (gw1 - delta) * scaling).astype(BF16)
        wb0 = w0.astype(BF16)
        wb1 = w1.astype(BF16)
        dks[h] = dot_nn(ds0, q).astype(BF16)
        dvs[h] = dot_nn(wb0, ga).astype(BF16)
        ol[h] = dot_tn(wb0, values) + dot_tn(wb1, v)
        dql[h] = dot_tn(ds0, keys) + dot_tn(ds1, k)
        dkl[h] = dot_nn(ds1, q)
        dvl[h] = dot_nn(wb1, ga)
        remote(dks.at[h], dkn.at[h], dk_ss.at[h], dk_rs.at[h], at(-1)).start()
        remote(dvs.at[h], dvn.at[h], dv_ss.at[h], dv_rs.at[h], at(-1)).start()
        return carry

    def local_heads(low, high):
        lax.fori_loop(low, high, local, 0)

    local_heads(0, 3)
    ring_out(fta, fro, fri, ftc, f_ss, f_rs, True)
    b_pair.wait_recv()
    combine(bx, bxp, btc, bta, b_ss, b_rs, is_early + is_late * m_before, is_late + is_early * m_before)
    local_heads(3, 6)
    spread(fta, fro, fri, fpo, fpc, f_ss, f_rs, True)
    ring_out(bta, bro, bri, btc, b_ss, b_rs, False)
    local_heads(6, 10)
    finish_start(
        fx, fxp, fpo, fpc, fsx, fres, f_ss, f_rs,
        is_late, is_early + is_late * m_before, is_early, is_late + is_early * m_before,
    )
    spread(bta, bro, bri, bpo, bpc, b_ss, b_rs, False)
    local_heads(10, HEADS)
    final(fsx, fres, f_ss, f_rs, False).wait_recv()

    def reads(h, carry):
        state = fres[place_of(h)]
        lifted = fq[h]
        den = den_s[h]
        inverse = 1.0 / jnp.maximum(den, 1.0)
        gate = gt[h]
        grad = g_s[:, columns(h)].astype(F32)
        out = dot_nn(lifted, state) * inverse
        near_out = ol[h]
        att_o[:, columns(h)] = (gate * out + (1.0 - gate) * near_out).astype(BF16)
        rows = jnp.sum(grad * (out - near_out), axis=0, keepdims=True)
        gg[h] = rows * (gate * (1.0 - gate))
        scaled_grad = grad * gate
        active = jnp.where(den > 1.0, 1.0, jnp.where(den == 1.0, 0.5, 0.0))
        dden = -jnp.sum(scaled_grad * out, axis=1, keepdims=True) * inverse * active
        back = dot_nt((scaled_grad * inverse).astype(BF16), state) + dden * zb[h]
        wide = lifted.astype(F32)
        dzt[h] = jnp.sum(dden * wide, axis=0, keepdims=True)
        dq_o[:, columns(h)] = (dql[h] + back * jnp.minimum(wide, 1.0)).astype(BF16)
        return carry

    lax.fori_loop(0, HEADS, reads, 0, unroll=2)
    for d in range(1, REACH + 1):
        remote(dzt, dzr.at[d - 1], dz_ss.at[d - 1], dz_rs.at[d - 1], at(-d)).start()

    lane = lax.broadcasted_iota(jnp.int32, (1, DIM), 1)
    mine = jnp.zeros((1, DIM), F32)
    for h in range(HEADS):
        mine = mine + jnp.where(lane == h, jnp.sum(gg[h], axis=1, keepdims=True), 0.0)
    red_s[0] = mine

    def row_copy(d):
        to = {"ctx": row * ROW + lax.rem(spot + d, ROW)}
        return remote(red_s.at[0], red_r.at[d - 1], red_ss.at[d - 1], red_rs.at[d - 1], to)

    for d in range(1, ROW):
        row_copy(d).start()
    copies_out = [
        pltpu.make_async_copy(att_o, att_out, out_sem.at[0]),
        pltpu.make_async_copy(dq_o, dq_out, out_sem.at[1]),
    ]
    for copy in copies_out:
        copy.start()

    finish_start(
        bx, bxp, bpo, bpc, bsx, bres, b_ss, b_rs,
        is_early, is_late + is_early * m_in, is_late, is_early + is_late * m_in,
    )
    for d in range(1, ROW):
        row_copy(d).wait_recv()
        mine = mine + red_r[d - 1]
    red_s[1] = mine

    n_rows = n_ctx // ROW

    def x_copy(d):
        i = ROW - 1 + d - 1
        return remote(red_s.at[1], red_r.at[i], red_ss.at[i], red_rs.at[i], at(ROW * d))

    for d in range(1, n_rows):
        x_copy(d).start()

    for d in range(1, REACH + 1):
        remote(dzt, dzr.at[d - 1], dz_ss.at[d - 1], dz_rs.at[d - 1], at(-d)).wait_recv()
    total = jnp.zeros((HEADS, 1, DIM), F32)
    for d in range(1, REACH + 1):
        weight = same(d - 1, 0) * (me + d < n_ctx).astype(F32)
        total = total + dzr[d - 1] * weight
    cz[...] = total

    for d in range(1, n_rows):
        x_copy(d).wait_recv()
        mine = mine + red_r[ROW - 1 + d - 1]

    def z_copy(i, d):
        j = ROW - 1 + n_rows - 1 + i
        return remote(red_s.at[2 + i], red_r.at[j], red_ss.at[j], red_rs.at[j], up(d))

    def z_begin(i):
        red_s[2 + i] = mine
        z_copy(i, steps_z[i]).start()

    def z_end(i):
        z_copy(i, steps_z[i]).wait_recv()
        return mine + red_r[ROW - 1 + n_rows - 1 + i]

    if steps_z:
        z_begin(0)
    final(bsx, bres, b_ss, b_rs, False).wait_recv()

    def writes(h, carry):
        remote(dks.at[h], dkn.at[h], dk_ss.at[h], dk_rs.at[h], at(-1)).wait_recv()
        remote(dvs.at[h], dvn.at[h], dv_ss.at[h], dv_rs.at[h], at(-1)).wait_recv()
        carried = bres[place_of(h)]
        lifted = fk[h]
        back = dot_nt(v_s[:, columns(h)], carried) + cz[h]
        mem_key = back * jnp.minimum(lifted.astype(F32), 1.0)
        dk_o[:, columns(h)] = (dkl[h] + dkn[h].astype(F32) + mem_key).astype(BF16)
        mem_value = dot_nn(lifted, carried)
        dv_o[:, columns(h)] = (dvl[h] + dvn[h].astype(F32) + mem_value).astype(BF16)
        return carry

    pieces = max(1, len(steps_z))
    for i in range(pieces):
        lax.fori_loop(i * HEADS // pieces, (i + 1) * HEADS // pieces, writes, 0)
        if steps_z:
            mine = z_end(i)
            if i + 1 < len(steps_z):
                z_begin(i + 1)
    gg_out[...] = mine[:, :HEADS]
    copies_out += [
        pltpu.make_async_copy(dk_o, dk_out, out_sem.at[2]),
        pltpu.make_async_copy(dv_o, dv_out, out_sem.at[3]),
    ]
    for copy in copies_out[2:]:
        copy.start()

    for i, d in enumerate(steps_z):
        z_copy(i, d).wait_send()
    for d in range(1, n_rows):
        x_copy(d).wait_send()
    for d in range(1, ROW):
        row_copy(d).wait_send()
    for d in range(1, REACH + 1):
        remote(zt, zr.at[d - 1], z_ss.at[d - 1], z_rs.at[d - 1], at(d)).wait_send()
        remote(dzt, dzr.at[d - 1], dz_ss.at[d - 1], dz_rs.at[d - 1], at(-d)).wait_send()
    for x, xp, tc, ta, ro, ri, po, pc, sx, res, ss, rs, forward in (
        (fx, fxp, ftc, fta, fro, fri, fpo, fpc, fsx, fres, f_ss, f_rs, True),
        (bx, bxp, btc, bta, bro, bri, bpo, bpc, bsx, bres, b_ss, b_rs, False),
    ):
        pair_send(x, xp, ss, rs).wait_send()
        for dy in range(1, 4):
            a2a(tc, ta, ss, rs, 1, dy, True).wait_send()
            a2a(po, pc, ss, rs, 5, dy, True).wait_send()
        remote(ro, ri, ss.at[4], rs.at[4], at(ROW if forward else -ROW)).wait_send()
        final(sx, res, ss, rs).wait_send()

    def drain(h, carry):
        remote(k_s.at[:, columns(h)], kp.at[h], k_ss.at[h], k_rs.at[h], at(1)).wait_send()
        remote(v_s.at[:, columns(h)], vp.at[h], v_ss.at[h], v_rs.at[h], at(1)).wait_send()
        remote(dks.at[h], dkn.at[h], dk_ss.at[h], dk_rs.at[h], at(-1)).wait_send()
        remote(dvs.at[h], dvn.at[h], dv_ss.at[h], dv_rs.at[h], at(-1)).wait_send()
        return carry

    lax.fori_loop(0, HEADS, drain, 0)
    for copy in copies_out:
        copy.wait()


def on_device(n_ctx, n_dp, queries, key_rows, value_rows, doc_ids, gate_logit, grad_out):
    flat = (SEG, HEADS * DIM)
    blocks = (HEADS, DIM, DIM)
    wide = jax.ShapeDtypeStruct(flat, BF16)
    anywhere = pl.BlockSpec(memory_space=pl.ANY)
    half = pltpu.VMEM(blocks, BF16)
    full = pltpu.VMEM(blocks, F32)

    def part(n):
        return pltpu.VMEM((n, DIM, DIM), BF16)

    lanes = pltpu.VMEM((HEADS, 1, DIM), F32)
    reach = pltpu.VMEM((REACH, HEADS, 1, DIM), F32)
    rows = pltpu.VMEM(flat, BF16)
    steps = max(1, n_dp.bit_length() - 1)
    n_red = ROW - 1 + n_ctx // ROW - 1 + steps
    exchange = [half, part(8), part(8), part(8), part(2), part(2), part(8), part(8), part(8), half]
    dma = pltpu.SemaphoreType.DMA
    scratch = (
        [rows] * 4
        + [pltpu.VMEM((2 * REACH + 1, 1, DIM), jnp.int32)]
        + [half] * 4 + [full]
        + exchange + exchange
        + [full] * 4 + [half] * 4
        + [rows] * 4
        + [lanes, reach, lanes, lanes, reach, lanes, lanes, lanes]
        + [pltpu.VMEM((2, SEG, SEG), F32), pltpu.VMEM((SEG, SEG), F32), pltpu.VMEM((SEG, DIM), F32)]
        + [pltpu.VMEM((2 + steps, 1, DIM), F32), pltpu.VMEM((n_red, 1, DIM), F32)]
        + [dma((5,)), dma((4,)), dma((15,)), dma((15,))]
        + [dma((REACH,))] * 4
        + [dma((HEADS,))] * 8
        + [dma((9,))] * 4
        + [dma((n_red,))] * 2
    )
    results = pl.pallas_call(
        functools.partial(kernel, n_ctx, n_dp),
        out_shape=[wide, wide, wide, wide, jax.ShapeDtypeStruct((1, HEADS), F32)],
        in_specs=[
            anywhere, anywhere, anywhere, anywhere,
            pl.BlockSpec(memory_space=pltpu.SMEM), anywhere,
        ],
        out_specs=[anywhere] * 4 + [pl.BlockSpec(memory_space=pltpu.VMEM)],
        scratch_shapes=scratch,
        compiler_params=pltpu.CompilerParams(
            collective_id=0, has_side_effects=True, vmem_limit_bytes=60 * 2**20
        ),
    )(
        queries.reshape(flat), key_rows.reshape(flat), value_rows.reshape(flat),
        doc_ids.reshape(1, SEG), gate_logit.reshape(1, HEADS), grad_out.reshape(flat),
    )
    shape = (1,) + flat
    return tuple(r.reshape(shape) for r in results[:4]) + (results[4].reshape(HEADS),)


def solution(mesh):
    tokens = P("dp", "ctx", None)
    return jax.shard_map(
        functools.partial(on_device, mesh.shape["ctx"], mesh.shape["dp"]),
        mesh=mesh,
        in_specs=(tokens, tokens, tokens, P("dp", "ctx"), P(), tokens),
        out_specs=(tokens, tokens, tokens, tokens, P()),
        check_vma=False,
    )
```

time: 634 us -> 95.5 us (0.15)
  the two profiles are of different devices: /device:TPU:1 before, /device:TPU:8 now
where the time goes in v1:
time: 95.5 us; the launch traced here: 95.2 us
  Pallas kernels  88.9 us (93%)
  local copies, waits for them, and re-layouts  5.71 us (6%)
    pallas_call x1, Pallas kernels, on_device(): pl.pallas_call(functools.partial(kernel, n_ctx, n_dp), out_shape=[wide, w...  88.9 us
    unnamed x13, local copies, waits for them, and re-layouts  5.71 us

profile of v1, /device:TPU:8, one launch (start us, length us, event | category | flops | bytes accessed | tf_op | source)
XLA Modules:
  0.0 95.2 jit_solution(16517230715072959649)
XLA Ops:
  0.6 88.9 %shard_map.101 = (bf16[128,2048]{1,0:T(8,128)(2,1)}, bf16[128,2048]{1,0:T(8,128)(2,1)}, bf16[128,2048]{1,0:T(8,128)(2,1)}, bf16[128,2048]{1,0:T(8,128)(2,1)}, f32[1,16]{1,0:T(1,128)}) custom-call(bf16[128,2048]{1,0:T(8,128)(2,1)} %bitcast.14, bf16[128,2048]{1,0:T(8,128)(2,1)} %bitcast.15, bf16[128,2048]{1,0:T(8,128)(2,1)} %bitcast.16, s32[1,128]{1,0:T(1,128)} %ids_in.1, ...), custom_call_target="tpu_custom_call" | custom-call | tf_op jit(solution)/shard_map/pallas_call | solution.py:498
  89.5 0.0 copy-start.2
  89.5 1.9 %copy.16 = bf16[1,128,2048]{2,1,0:T(8,128)(2,1)} copy(bf16[1,128,2048]{2,1,0:T(8,128)(2,1)} %bitcast.13) | data formatting | bytes 1048576
  91.5 0.0 copy-done.2
  91.5 0.0 copy-start.1
  91.5 0.8 copy.17
  92.3 0.4 copy-done.1
  92.7 0.0 copy-start
  92.7 0.8 copy.18
  93.5 0.4 copy-done
  93.9 0.0 copy-start.3
  93.9 0.8 copy.19
  94.7 0.0 copy-done.3
  94.7 0.5 copy.20
Async XLA Ops:
  89.5 2.0 %copy-start.2 = (bf16[128,2048]{1,0:T(8,128)(2,1)S(1)}, bf16[128,2048]{1,0:T(8,128)(2,1)}, u32[]{:S(2)}) copy-start(bf16[128,2048]{1,0:T(8,128)(2,1)} %get-tuple-element.11) | copy-start | bytes 1572868
  91.5 1.2 %copy-start.1 = (bf16[128,2048]{1,0:T(8,128)(2,1)S(1)}, bf16[128,2048]{1,0:T(8,128)(2,1)}, u32[]{:S(2)}) copy-start(bf16[128,2048]{1,0:T(8,128)(2,1)} %get-tuple-element.12) | copy-start | bytes 1572868
  92.7 1.2 %copy-start = (bf16[128,2048]{1,0:T(8,128)(2,1)S(1)}, bf16[128,2048]{1,0:T(8,128)(2,1)}, u32[]{:S(2)}) copy-start(bf16[128,2048]{1,0:T(8,128)(2,1)} %get-tuple-element.13) | copy-start | bytes 1572868
  93.9 0.8 copy-start.3

commit v2 on v1

--- a/solution.py
+++ b/solution.py
@@ -13,6 +13,8 @@
 HEADS = 16
 ROW = 8
 REACH = 8
+UNROLL = 2
+SCOPED = 103 * 2**19
 MESH = pl.DeviceIdType.MESH
 F32 = jnp.float32
 BF16 = jnp.bfloat16
@@ -46,14 +48,13 @@
     n_ctx, n_dp,
     q_in, k_in, v_in, ids_in, gate_in, g_in,
     att_out, dq_out, dk_out, dv_out, gg_out,
-    q_s, k_s, v_s, g_s, idr, kp, vp, fk, fq, den_s,
+    q_s, k_s, v_s, g_s, idr, kp, vp, fk, fq, inv_s, den_s,
     fx, fxp, ftc, fta, fro, fri, fpo, fpc, fsx, fres,
     bx, bxp, btc, bta, bro, bri, bpo, bpc, bsx, bres,
-    ol, dql, dkl, dvl, dks, dvs, dkn, dvn,
-    att_o, dq_o, dk_o, dv_o,
+    ol, dql, dkl, dvl, dks, dvs, dkn, dvn, att_o, dq_o, dk_o, dv_o,
     zt, zr, zb, dzt, dzr, cz, gt, gg, bias, wm, um,
     red_s, red_r,
-    load_sem, out_sem, ids_ss, ids_rs, z_ss, z_rs, dz_ss, dz_rs,
+    load_sem, out_sem, ready, ids_ss, ids_rs, z_ss, z_rs, dz_ss, dz_rs,
     k_ss, k_rs, v_ss, v_rs, dk_ss, dk_rs, dv_ss, dv_rs,
     f_ss, f_rs, b_ss, b_rs, red_ss, red_rs,
 ):
@@ -76,59 +77,77 @@
             device_id=device, device_id_type=MESH,
         )
 
+    quarter = HEADS * DIM // 4
     loads = []
-    for i, (src, dst) in enumerate(
-        ((ids_in, idr.at[REACH]), (k_in, k_s), (v_in, v_s), (q_in, q_s), (g_in, g_s))
-    ):
-        copy = pltpu.make_async_copy(src, dst, load_sem.at[i])
+    for i in range(4):
+        part = pl.ds(i * quarter, quarter)
+        loads.append(pltpu.make_async_copy(k_in.at[:, part], k_s.at[:, part], load_sem.at[i]))
+    for i, (src, dst) in enumerate(((ids_in, idr.at[REACH]), (v_in, v_s), (q_in, q_s), (g_in, g_s))):
+        loads.append(pltpu.make_async_copy(src, dst, load_sem.at[4 + i]))
+    for copy in loads[4:5] + loads[:4]:
         copy.start()
-        loads.append(copy)
     barrier = pltpu.get_barrier_semaphore()
     near = [d for d in range(-REACH, REACH + 1) if d] + [n_ctx // 2]
-    steps_z = []
-    d = 1
-    while d < n_dp:
-        steps_z.append(d)
-        d *= 2
-    far = sorted({s % n_dp for d in steps_z for s in (d, -d)})
+    far = [1, n_dp - 1] if n_dp > 2 else []
+    hops = list(range(1, n_dp)) if far else []
     for d in near:
         pl.semaphore_signal(barrier, inc=1, device_id=at(d), device_id_type=MESH)
     for d in far:
         pl.semaphore_signal(barrier, inc=1, device_id=up(d), device_id_type=MESH)
 
+    loads[5].start()
     for h in range(HEADS):
         logit = jnp.full((1, DIM), gate_in[0, h], F32)
         gt[h] = 1.0 / (1.0 + jnp.exp(-logit))
-    loads[0].wait()
+    loads[4].wait()
     own_ids = idr[REACH]
     own_cols = jnp.broadcast_to(own_ids.astype(F32), (SEG, SEG))
     own_rows = jnp.transpose(own_cols)
     own_last = own_ids[:, SEG - 1 :].astype(F32)
     wm[...] = (own_rows == own_last).astype(F32)
-    loads[1].wait()
-    loads[2].wait()
+    def lift(h, carry):
+        lifted = feature(k_s[:, columns(h)].astype(F32)) * wm[...]
+        fk[h] = lifted.astype(BF16)
+        zt[h] = jnp.sum(lifted, axis=0, keepdims=True)
+        return carry
+
+    for i in range(4):
+        loads[i].wait()
+        lax.fori_loop(4 * i, 4 * i + 4, lift, 0, unroll=4)
+    for copy in loads[6:]:
+        copy.start()
     pl.semaphore_wait(barrier, len(near) + len(far))
 
     id_sends = [d for d in range(-(REACH - 1), REACH + 1) if d]
     for i, d in enumerate(id_sends):
         remote(idr.at[REACH], idr.at[REACH - d], ids_ss.at[i], ids_rs.at[i], at(d)).start()
+    for d in range(1, REACH + 1):
+        remote(zt, zr.at[d - 1], z_ss.at[d - 1], z_rs.at[d - 1], at(d)).start()
+    def tell(i):
+        if far:
+            for d in (2**i, -(2**i)):
+                pl.semaphore_signal(ready.at[i], inc=1, device_id=up(d), device_id_type=MESH)
+
+    def told(i):
+        if far:
+            pl.semaphore_wait(ready.at[i], 2)
+
+    tell(0)
 
     def send_kv(h, carry):
         remote(k_s.at[:, columns(h)], kp.at[h], k_ss.at[h], k_rs.at[h], at(1)).start()
         remote(v_s.at[:, columns(h)], vp.at[h], v_ss.at[h], v_rs.at[h], at(1)).start()
         return carry
 
-    lax.fori_loop(0, HEADS, send_kv, 0)
+    loads[5].wait()
+    for h in range(4):
+        send_kv(h, 0)
 
     def tails(h, carry):
-        lifted = feature(k_s[:, columns(h)].astype(F32)) * wm[...]
-        short = lifted.astype(BF16)
-        fk[h] = short
-        zt[h] = jnp.sum(lifted, axis=0, keepdims=True)
-        fx[place_of(h)] = dot_tn(short, v_s[:, columns(h)]).astype(BF16)
-        return carry
-
-    lax.fori_loop(0, HEADS, tails, 0, unroll=2)
+        fx[place_of(h)] = dot_tn(fk[h], v_s[:, columns(h)]).astype(BF16)
+        return carry
+
+    lax.fori_loop(0, HEADS, tails, 0, unroll=4)
 
     def pair_send(x, xp, ss, rs):
         other = pl.ds(pl.multiple_of((1 - core) * 8, 8), 8)
@@ -136,11 +155,13 @@
 
     f_pair = pair_send(fx, fxp, f_ss, f_rs)
     f_pair.start()
-    for d in range(1, REACH + 1):
-        remote(zt, zr.at[d - 1], z_ss.at[d - 1], z_rs.at[d - 1], at(d)).start()
-
-    for i, d in enumerate(id_sends):
-        remote(idr.at[REACH], idr.at[REACH - d], ids_ss.at[i], ids_rs.at[i], at(d)).wait()
+
+    def await_ids(near_by):
+        for i, d in enumerate(id_sends):
+            if (abs(d) == 1) == near_by:
+                remote(idr.at[REACH], idr.at[REACH - d], ids_ss.at[i], ids_rs.at[i], at(d)).wait()
+
+    await_ids(True)
 
     def last(offset):
         return idr[REACH + offset][:, SEG - 1 :]
@@ -155,11 +176,13 @@
     last_row = (row < n_ctx // ROW - 1).astype(F32)
     early, late, before = -core, 1 - core, -1 - core
     m_in = same(early, late)
-    m_before = same(early, before) * (me - core > 0).astype(F32)
-    kappa = []
-    for c in range(4):
-        value = same(2 * c + 1 - spot, 2 * c - 1 - spot)
-        kappa.append(value * first_chip if c == 0 else value)
+
+    def far_masks():
+        kappa = []
+        for c in range(4):
+            value = same(2 * c + 1 - spot, 2 * c - 1 - spot)
+            kappa.append(value * first_chip if c == 0 else value)
+        return kappa, same(early, before) * (me - core > 0).astype(F32)
 
     prev_ids = idr[REACH - 1]
     prev_rows = jnp.transpose(jnp.broadcast_to(prev_ids.astype(F32), (SEG, SEG)))
@@ -232,37 +255,12 @@
 
     f_pair.wait_recv()
     combine(fx, fxp, ftc, fta, f_ss, f_rs, is_late + is_early * m_in, is_early + is_late * m_in)
-
-    for d in range(1, REACH + 1):
-        remote(zt, zr.at[d - 1], z_ss.at[d - 1], z_rs.at[d - 1], at(d)).wait_recv()
-    total = jnp.zeros((HEADS, 1, DIM), F32)
-    for d in range(1, REACH + 1):
-        weight = same(-d, -1) * (me >= d).astype(F32)
-        total = total + zr[d - 1] * weight
-    zb[...] = total
-    loads[3].wait()
-    loads[4].wait()
-
-    def state_part(h, carry):
-        lifted = (feature(q_s[:, columns(h)].astype(F32)) * um[...]).astype(BF16)
-        fq[h] = lifted
-        totals = jnp.broadcast_to(zb[h], (DIM, DIM)).astype(BF16)
-        den = dot_nt(lifted, totals)
-        den_s[h] = den
-        scaled = g_s[:, columns(h)].astype(F32) * gt[h] / jnp.maximum(den, 1.0)
-        bx[place_of(h)] = dot_tn(lifted, scaled.astype(BF16)).astype(BF16)
-        return carry
-
-    lax.fori_loop(0, HEADS, state_part, 0, unroll=2)
-    b_pair = pair_send(bx, bxp, b_ss, b_rs)
-    b_pair.start()
-
+    loads[6].wait()
+    loads[7].wait()
     scaling = DIM ** -0.5
     scale2 = scaling * math.log2(math.e)
 
     def local(h, carry):
-        remote(k_s.at[:, columns(h)], kp.at[h], k_ss.at[h], k_rs.at[h], at(1)).wait_recv()
-        remote(v_s.at[:, columns(h)], vp.at[h], v_ss.at[h], v_rs.at[h], at(1)).wait_recv()
         q = q_s[:, columns(h)]
         k = k_s[:, columns(h)]
         v = v_s[:, columns(h)]
@@ -285,94 +283,173 @@
         wb1 = w1.astype(BF16)
         dks[h] = dot_nn(ds0, q).astype(BF16)
         dvs[h] = dot_nn(wb0, ga).astype(BF16)
-        ol[h] = dot_tn(wb0, values) + dot_tn(wb1, v)
+        out = dot_tn(wb0, values) + dot_tn(wb1, v)
+        ol[h] = out
+        gate = gt[h]
+        rows = jnp.sum(g_s[:, columns(h)].astype(F32) * out, axis=0, keepdims=True)
+        gg[h] = rows * (gate * (gate - 1.0))
         dql[h] = dot_tn(ds0, keys) + dot_tn(ds1, k)
         dkl[h] = dot_nn(ds1, q)
         dvl[h] = dot_nn(wb1, ga)
+        return carry
+
+    def send_back(h, carry):
         remote(dks.at[h], dkn.at[h], dk_ss.at[h], dk_rs.at[h], at(-1)).start()
         remote(dvs.at[h], dvn.at[h], dv_ss.at[h], dv_rs.at[h], at(-1)).start()
         return carry
 
-    def local_heads(low, high):
-        lax.fori_loop(low, high, local, 0)
-
-    local_heads(0, 3)
+    def arrived(h, carry):
+        remote(k_s.at[:, columns(h)], kp.at[h], k_ss.at[h], k_rs.at[h], at(1)).wait_recv()
+        remote(v_s.at[:, columns(h)], vp.at[h], v_ss.at[h], v_rs.at[h], at(1)).wait_recv()
+        return carry
+
+    def local_heads(low, more=()):
+        for h in range(low, low + 2):
+            arrived(h, 0)
+        lax.fori_loop(low, low + 2, local, 0, unroll=UNROLL)
+        for h in range(low, low + 2):
+            send_back(h, 0)
+        for h in more:
+            send_kv(h, 0)
+
+    await_ids(False)
+    kappa, m_before = far_masks()
+    told(0)
+    tell(1)
+
+    for d in range(1, REACH + 1):
+        remote(zt, zr.at[d - 1], z_ss.at[d - 1], z_rs.at[d - 1], at(d)).wait_recv()
+    total = jnp.zeros((HEADS, 1, DIM), F32)
+    for d in range(1, REACH + 1):
+        weight = same(-d, -1) * (me >= d).astype(F32)
+        total = total + zr[d - 1] * weight
+    zb[...] = total
+
+    def state_part(h, carry):
+        lifted = (feature(q_s[:, columns(h)].astype(F32)) * um[...]).astype(BF16)
+        fq[h] = lifted
+        totals = jnp.broadcast_to(zb[h], (DIM, DIM)).astype(BF16)
+        den = dot_nt(lifted, totals)
+        inverse = 1.0 / jnp.maximum(den, 1.0)
+        inv_s[h] = inverse
+        den_s[h] = den
+        scaled = g_s[:, columns(h)].astype(F32) * gt[h] * inverse
+        bx[place_of(h)] = dot_tn(lifted, scaled.astype(BF16)).astype(BF16)
+        return carry
+
+    for i in range(4):
+        lax.fori_loop(4 * i, 4 * i + 4, state_part, 0, unroll=4)
+        send_kv(4 + i, 0)
+    b_pair = pair_send(bx, bxp, b_ss, b_rs)
+    b_pair.start()
+
+    def add_rows(h, rows):
+        gg[h] = gg[h] + rows * (1.0 - gt[h])
+
     ring_out(fta, fro, fri, ftc, f_ss, f_rs, True)
+    local_heads(0, (8,))
     b_pair.wait_recv()
     combine(bx, bxp, btc, bta, b_ss, b_rs, is_early + is_late * m_before, is_late + is_early * m_before)
-    local_heads(3, 6)
+    send_kv(9, 0)
+    local_heads(2, (10,))
+    told(1)
+    tell(2)
+    local_heads(4, (11,))
     spread(fta, fro, fri, fpo, fpc, f_ss, f_rs, True)
+    local_heads(6, (12, 13))
+    local_heads(8, (14, 15))
     ring_out(bta, bro, bri, btc, b_ss, b_rs, False)
-    local_heads(6, 10)
+    local_heads(10)
+    local_heads(12)
+    spread(bta, bro, bri, bpo, bpc, b_ss, b_rs, False)
+    local_heads(14)
+
+    for i in range(2):
+        rows = jnp.zeros((1, DIM), F32)
+        for c in range(4):
+            product = bta[2 * c + i].astype(F32) * fpo[2 * c + i].astype(F32)
+            rows = rows + jnp.sum(product, axis=0, keepdims=True)
+        add_rows(2 * spot + i, rows)
+    late_core = core == 1
+    for i in range(8):
+        grads = jnp.where(late_core, bx[core * 8 + i], bxp[i]).astype(F32)
+        states = jnp.where(late_core, fxp[i], fx[core * 8 + i]).astype(F32)
+        rows = jnp.sum(grads * states, axis=0, keepdims=True)
+        add_rows(4 * (i // 2) + 2 * core + i % 2, rows)
+
+    lane = lax.broadcasted_iota(jnp.int32, (1, DIM), 1)
+    mine = jnp.zeros((1, DIM), F32)
+    for h in range(HEADS):
+        mine = mine + jnp.where(lane == h, jnp.sum(gg[h], axis=1, keepdims=True), 0.0)
+    red_s[0] = mine
+
+    n_rows = n_ctx // ROW
+
+    def x_copy(d):
+        i = d - 1
+        return remote(red_s.at[0], red_r.at[i], red_ss.at[i], red_rs.at[i], at(ROW * d))
+
+    def z_copy(d):
+        j = n_rows - 1 + d - 1
+        return remote(red_s.at[1], red_r.at[j], red_ss.at[j], red_rs.at[j], up(d))
+
+    def row_copy(d):
+        to = {"ctx": row * ROW + lax.rem(spot + d, ROW)}
+        j = n_rows - 1 + n_dp - 1 + d - 1
+        return remote(red_s.at[2], red_r.at[j], red_ss.at[j], red_rs.at[j], to)
+
+    for d in range(1, n_rows):
+        x_copy(d).start()
     finish_start(
         fx, fxp, fpo, fpc, fsx, fres, f_ss, f_rs,
         is_late, is_early + is_late * m_before, is_early, is_late + is_early * m_before,
     )
-    spread(bta, bro, bri, bpo, bpc, b_ss, b_rs, False)
-    local_heads(10, HEADS)
+    told(2)
+    for d in range(1, n_rows):
+        x_copy(d).wait_recv()
+        mine = mine + red_r[d - 1]
+    red_s[1] = mine
+    for d in hops:
+        z_copy(d).start()
     final(fsx, fres, f_ss, f_rs, False).wait_recv()
 
     def reads(h, carry):
         state = fres[place_of(h)]
         lifted = fq[h]
-        den = den_s[h]
-        inverse = 1.0 / jnp.maximum(den, 1.0)
+        inverse = inv_s[h]
         gate = gt[h]
         grad = g_s[:, columns(h)].astype(F32)
         out = dot_nn(lifted, state) * inverse
         near_out = ol[h]
         att_o[:, columns(h)] = (gate * out + (1.0 - gate) * near_out).astype(BF16)
-        rows = jnp.sum(grad * (out - near_out), axis=0, keepdims=True)
-        gg[h] = rows * (gate * (1.0 - gate))
         scaled_grad = grad * gate
-        active = jnp.where(den > 1.0, 1.0, jnp.where(den == 1.0, 0.5, 0.0))
-        dden = -jnp.sum(scaled_grad * out, axis=1, keepdims=True) * inverse * active
+        den = den_s[h]
+        active = jnp.where(den > 1.0, inverse, jnp.where(den == 1.0, 0.5, 0.0))
+        dden = -jnp.sum(scaled_grad * out, axis=1, keepdims=True) * active
         back = dot_nt((scaled_grad * inverse).astype(BF16), state) + dden * zb[h]
         wide = lifted.astype(F32)
         dzt[h] = jnp.sum(dden * wide, axis=0, keepdims=True)
         dq_o[:, columns(h)] = (dql[h] + back * jnp.minimum(wide, 1.0)).astype(BF16)
         return carry
 
-    lax.fori_loop(0, HEADS, reads, 0, unroll=2)
+    lax.fori_loop(0, HEADS, reads, 0, unroll=4)
     for d in range(1, REACH + 1):
         remote(dzt, dzr.at[d - 1], dz_ss.at[d - 1], dz_rs.at[d - 1], at(-d)).start()
 
-    lane = lax.broadcasted_iota(jnp.int32, (1, DIM), 1)
-    mine = jnp.zeros((1, DIM), F32)
-    for h in range(HEADS):
-        mine = mine + jnp.where(lane == h, jnp.sum(gg[h], axis=1, keepdims=True), 0.0)
-    red_s[0] = mine
-
-    def row_copy(d):
-        to = {"ctx": row * ROW + lax.rem(spot + d, ROW)}
-        return remote(red_s.at[0], red_r.at[d - 1], red_ss.at[d - 1], red_rs.at[d - 1], to)
-
-    for d in range(1, ROW):
-        row_copy(d).start()
-    copies_out = [
-        pltpu.make_async_copy(att_o, att_out, out_sem.at[0]),
-        pltpu.make_async_copy(dq_o, dq_out, out_sem.at[1]),
-    ]
-    for copy in copies_out:
-        copy.start()
-
+    half = HEADS * DIM // 2
+
+    def put(i, which):
+        src, dst = ((att_o, att_out), (dq_o, dq_out), (dk_o, dk_out), (dv_o, dv_out))[which]
+        part = pl.ds(i * half, half)
+        return pltpu.make_async_copy(src.at[:, part], dst.at[:, part], out_sem.at[2 * which + i])
+
+    for i in range(2):
+        put(i, 0).start()
+        put(i, 1).start()
     finish_start(
         bx, bxp, bpo, bpc, bsx, bres, b_ss, b_rs,
         is_early, is_late + is_early * m_in, is_late, is_early + is_late * m_in,
     )
-    for d in range(1, ROW):
-        row_copy(d).wait_recv()
-        mine = mine + red_r[d - 1]
-    red_s[1] = mine
-
-    n_rows = n_ctx // ROW
-
-    def x_copy(d):
-        i = ROW - 1 + d - 1
-        return remote(red_s.at[1], red_r.at[i], red_ss.at[i], red_rs.at[i], at(ROW * d))
-
-    for d in range(1, n_rows):
-        x_copy(d).start()
 
     for d in range(1, REACH + 1):
         remote(dzt, dzr.at[d - 1], dz_ss.at[d - 1], dz_rs.at[d - 1], at(-d)).wait_recv()
@@ -382,29 +459,9 @@
         total = total + dzr[d - 1] * weight
     cz[...] = total
 
-    for d in range(1, n_rows):
-        x_copy(d).wait_recv()
-        mine = mine + red_r[ROW - 1 + d - 1]
-
-    def z_copy(i, d):
-        j = ROW - 1 + n_rows - 1 + i
-        return remote(red_s.at[2 + i], red_r.at[j], red_ss.at[j], red_rs.at[j], up(d))
-
-    def z_begin(i):
-        red_s[2 + i] = mine
-        z_copy(i, steps_z[i]).start()
-
-    def z_end(i):
-        z_copy(i, steps_z[i]).wait_recv()
-        return mine + red_r[ROW - 1 + n_rows - 1 + i]
-
-    if steps_z:
-        z_begin(0)
     final(bsx, bres, b_ss, b_rs, False).wait_recv()
 
     def writes(h, carry):
-        remote(dks.at[h], dkn.at[h], dk_ss.at[h], dk_rs.at[h], at(-1)).wait_recv()
-        remote(dvs.at[h], dvn.at[h], dv_ss.at[h], dv_rs.at[h], at(-1)).wait_recv()
         carried = bres[place_of(h)]
         lifted = fk[h]
         back = dot_nt(v_s[:, columns(h)], carried) + cz[h]
@@ -414,23 +471,30 @@
         dv_o[:, columns(h)] = (dvl[h] + dvn[h].astype(F32) + mem_value).astype(BF16)
         return carry
 
-    pieces = max(1, len(steps_z))
-    for i in range(pieces):
-        lax.fori_loop(i * HEADS // pieces, (i + 1) * HEADS // pieces, writes, 0)
-        if steps_z:
-            mine = z_end(i)
-            if i + 1 < len(steps_z):
-                z_begin(i + 1)
+    def returned(h, carry):
+        remote(dks.at[h], dkn.at[h], dk_ss.at[h], dk_rs.at[h], at(-1)).wait_recv()
+        remote(dvs.at[h], dvn.at[h], dv_ss.at[h], dv_rs.at[h], at(-1)).wait_recv()
+        return carry
+
+    for i in range(2):
+        low, high = i * HEADS // 2, (i + 1) * HEADS // 2
+        lax.fori_loop(low, high, returned, 0)
+        lax.fori_loop(low, high, writes, 0, unroll=4)
+        put(i, 2).start()
+        put(i, 3).start()
+    for d in hops:
+        z_copy(d).wait_recv()
+        mine = mine + red_r[n_rows - 1 + d - 1]
+    red_s[2] = mine
+    for d in range(1, ROW):
+        row_copy(d).start()
+    for d in range(1, ROW):
+        row_copy(d).wait_recv()
+        mine = mine + red_r[n_rows - 1 + n_dp - 1 + d - 1]
     gg_out[...] = mine[:, :HEADS]
-    copies_out += [
-        pltpu.make_async_copy(dk_o, dk_out, out_sem.at[2]),
-        pltpu.make_async_copy(dv_o, dv_out, out_sem.at[3]),
-    ]
-    for copy in copies_out[2:]:
-        copy.start()
-
-    for i, d in enumerate(steps_z):
-        z_copy(i, d).wait_send()
+
+    for d in hops:
+        z_copy(d).wait_send()
     for d in range(1, n_rows):
         x_copy(d).wait_send()
     for d in range(1, ROW):
@@ -457,7 +521,17 @@
         return carry
 
     lax.fori_loop(0, HEADS, drain, 0)
-    for copy in copies_out:
+    for i in range(2):
+        for which in range(4):
+            put(i, which).wait()
+
+
+def write_out(*refs):
+    ins, outs, sem = refs[:5], refs[5:10], refs[10]
+    copies = [pltpu.make_async_copy(a, b, sem.at[i]) for i, (a, b) in enumerate(zip(ins, outs))]
+    for copy in copies:
+        copy.start()
+    for copy in copies:
         copy.wait()
 
 
@@ -465,7 +539,9 @@
     flat = (SEG, HEADS * DIM)
     blocks = (HEADS, DIM, DIM)
     wide = jax.ShapeDtypeStruct(flat, BF16)
-    anywhere = pl.BlockSpec(memory_space=pl.ANY)
+    anywhere = pl.BlockSpec(memory_space=pltpu.HBM)
+    vmem = pl.BlockSpec(memory_space=pltpu.VMEM)
+    free = pl.BlockSpec(memory_space=pl.ANY)
     half = pltpu.VMEM(blocks, BF16)
     full = pltpu.VMEM(blocks, F32)
 
@@ -475,44 +551,51 @@
     lanes = pltpu.VMEM((HEADS, 1, DIM), F32)
     reach = pltpu.VMEM((REACH, HEADS, 1, DIM), F32)
     rows = pltpu.VMEM(flat, BF16)
-    steps = max(1, n_dp.bit_length() - 1)
-    n_red = ROW - 1 + n_ctx // ROW - 1 + steps
+    n_red = ROW - 1 + n_ctx // ROW - 1 + n_dp - 1
     exchange = [half, part(8), part(8), part(8), part(2), part(2), part(8), part(8), part(8), half]
     dma = pltpu.SemaphoreType.DMA
     scratch = (
         [rows] * 4
         + [pltpu.VMEM((2 * REACH + 1, 1, DIM), jnp.int32)]
-        + [half] * 4 + [full]
+        + [half] * 4 + [full] * 2
         + exchange + exchange
-        + [full] * 4 + [half] * 4
-        + [rows] * 4
+        + [full] * 4 + [half] * 4 + [rows] * 4
         + [lanes, reach, lanes, lanes, reach, lanes, lanes, lanes]
         + [pltpu.VMEM((2, SEG, SEG), F32), pltpu.VMEM((SEG, SEG), F32), pltpu.VMEM((SEG, DIM), F32)]
-        + [pltpu.VMEM((2 + steps, 1, DIM), F32), pltpu.VMEM((n_red, 1, DIM), F32)]
-        + [dma((5,)), dma((4,)), dma((15,)), dma((15,))]
+        + [pltpu.VMEM((3, 1, DIM), F32), pltpu.VMEM((n_red, 1, DIM), F32)]
+        + [dma((8,)), dma((8,)), pltpu.SemaphoreType.REGULAR((3,)), dma((15,)), dma((15,))]
         + [dma((REACH,))] * 4
         + [dma((HEADS,))] * 8
         + [dma((9,))] * 4
         + [dma((n_red,))] * 2
     )
+    shapes = [wide] * 4 + [jax.ShapeDtypeStruct((1, HEADS), F32)]
     results = pl.pallas_call(
         functools.partial(kernel, n_ctx, n_dp),
-        out_shape=[wide, wide, wide, wide, jax.ShapeDtypeStruct((1, HEADS), F32)],
+        out_shape=shapes,
         in_specs=[
             anywhere, anywhere, anywhere, anywhere,
             pl.BlockSpec(memory_space=pltpu.SMEM), anywhere,
         ],
-        out_specs=[anywhere] * 4 + [pl.BlockSpec(memory_space=pltpu.VMEM)],
+        out_specs=[free] * 4 + [vmem],
         scratch_shapes=scratch,
         compiler_params=pltpu.CompilerParams(
-            collective_id=0, has_side_effects=True, vmem_limit_bytes=60 * 2**20
+            collective_id=0, has_side_effects=True, vmem_limit_bytes=SCOPED
         ),
     )(
         queries.reshape(flat), key_rows.reshape(flat), value_rows.reshape(flat),
         doc_ids.reshape(1, SEG), gate_logit.reshape(1, HEADS), grad_out.reshape(flat),
     )
+    written = pl.pallas_call(
+        write_out,
+        out_shape=shapes,
+        in_specs=[vmem] * 5,
+        out_specs=[anywhere] * 5,
+        scratch_shapes=[dma((5,))],
+        compiler_params=pltpu.CompilerParams(vmem_limit_bytes=2**20),
+    )(*results)
     shape = (1,) + flat
-    return tuple(r.reshape(shape) for r in results[:4]) + (results[4].reshape(HEADS),)
+    return tuple(r.reshape(shape) for r in written[:4]) + (written[4].reshape(HEADS),)
 
 
 def solution(mesh):

time: 95.5 us -> 69.1 us (0.72)
  the two profiles are of different devices: /device:TPU:8 before, /device:TPU:1 now
where the time goes in v2:
time: 69.1 us; the launch traced here: 69 us
  Pallas kernels  67.6 us (98%)
    pallas_call x1, Pallas kernels, on_device(): pl.pallas_call(functools.partial(kernel, n_ctx, n_dp), out_shape=shapes,...  66.3 us

profile of v2, /device:TPU:1, one launch (start us, length us, event | category | flops | bytes accessed | tf_op | source)
XLA Modules:
  0.0 69.0 jit_solution(13641208569444440550)
XLA Ops:
  0.6 0.0 copy-start
  0.6 0.0 copy-start.1
  0.7 0.6 copy-done
  1.3 0.0 copy-done.1
  1.3 66.3 %shard_map.101 = (bf16[128,2048]{1,0:T(8,128)(2,1)S(1)}, bf16[128,2048]{1,0:T(8,128)(2,1)S(1)}, bf16[128,2048]{1,0:T(8,128)(2,1)S(1)}, bf16[128,2048]{1,0:T(8,128)(2,1)S(1)}, f32[1,16]{1,0:T(1,128)S(1)}) custom-call(bf16[128,2048]{1,0:T(8,128)(2,1)} %bitcast.11, bf16[128,2048]{1,0:T(8,128)(2,1)} %bitcast.12, bf16[128,2048]{1,0:T(8,128)(2,1)} %bitcast.13, ...), custom_call_target="tpu_custom_call" | custom-call | tf_op jit(solution)/shard_map/pallas_call | solution.py:573
  67.6 1.4 %shard_map.102 = (bf16[128,2048]{1,0:T(8,128)(2,1)}, bf16[128,2048]{1,0:T(8,128)(2,1)}, bf16[128,2048]{1,0:T(8,128)(2,1)}, bf16[128,2048]{1,0:T(8,128)(2,1)}, f32[1,16]{1,0:T(1,128)}) custom-call(bf16[128,2048]{1,0:T(8,128)(2,1)S(1)} %get-tuple-element.15.refs_0_, bf16[128,2048]{1,0:T(8,128)(2,1)S(1)} %get-tuple-element.16.refs_1_, ...), custom_call_target="tpu_custom_call" | custom-call | tf_op jit(solution)/shard_map/pallas_call | solution.py:589
Async XLA Ops:
  0.6 0.7 copy-start
  0.6 0.7 copy-start.1

commit v3 on v2

--- a/solution.py
+++ b/solution.py
@@ -14,6 +14,8 @@
 ROW = 8
 REACH = 8
 UNROLL = 2
+KV_AT = {"start": (0, 1), "f1": (2, 3, 4, 5), "s2": (6,), "b1": (7, 8, 9), "f2": (10, 11, 12), "l8": (13, 14, 15)}
+BACK_AT = {f"l{h}": (h, h + 1) for h in range(0, 16, 2)}
 SCOPED = 103 * 2**19
 MESH = pl.DeviceIdType.MESH
 F32 = jnp.float32
@@ -48,15 +50,14 @@
     n_ctx, n_dp,
     q_in, k_in, v_in, ids_in, gate_in, g_in,
     att_out, dq_out, dk_out, dv_out, gg_out,
-    q_s, k_s, v_s, g_s, idr, kp, vp, fk, fq, inv_s, den_s,
+    q_s, k_s, v_s, g_s, idr, kvp, fk, fq, inv_s, den_s,
     fx, fxp, ftc, fta, fro, fri, fpo, fpc, fsx, fres,
     bx, bxp, btc, bta, bro, bri, bpo, bpc, bsx, bres,
-    ol, dql, dkl, dvl, dks, dvs, dkn, dvn, att_o, dq_o, dk_o, dv_o,
+    ol, dql, dkl, dvl, dks, dvs, dkvn, att_o, dq_o, dk_o, dv_o,
     zt, zr, zb, dzt, dzr, cz, gt, gg, bias, wm, um,
     red_s, red_r,
-    load_sem, out_sem, ready, ids_ss, ids_rs, z_ss, z_rs, dz_ss, dz_rs,
-    k_ss, k_rs, v_ss, v_rs, dk_ss, dk_rs, dv_ss, dv_rs,
-    f_ss, f_rs, b_ss, b_rs, red_ss, red_rs,
+    load_sem, out_sem, ready, sent, ids_rs, z_rs, dz_rs, kv_rs, dkv_rs,
+    f_ss, f_rs, b_ss, b_rs, red_rs,
 ):
     me = lax.axis_index("ctx")
     mz = lax.axis_index("dp")
@@ -76,6 +77,9 @@
             src_ref=src, dst_ref=dst, send_sem=ss, recv_sem=rs,
             device_id=device, device_id_type=MESH,
         )
+
+    def arrival(ref, sem):
+        pltpu.make_async_copy(ref, ref, sem).wait()
 
     quarter = HEADS * DIM // 4
     loads = []
@@ -120,9 +124,10 @@
 
     id_sends = [d for d in range(-(REACH - 1), REACH + 1) if d]
     for i, d in enumerate(id_sends):
-        remote(idr.at[REACH], idr.at[REACH - d], ids_ss.at[i], ids_rs.at[i], at(d)).start()
+        which = {1: 0, -1: 1}.get(d, 2)
+        remote(idr.at[REACH], idr.at[REACH - d], sent.at[2], ids_rs.at[which], at(d)).start()
     for d in range(1, REACH + 1):
-        remote(zt, zr.at[d - 1], z_ss.at[d - 1], z_rs.at[d - 1], at(d)).start()
+        remote(zt, zr.at[d - 1], sent.at[3], z_rs, at(d)).start()
     def tell(i):
         if far:
             for d in (2**i, -(2**i)):
@@ -135,13 +140,23 @@
     tell(0)
 
     def send_kv(h, carry):
-        remote(k_s.at[:, columns(h)], kp.at[h], k_ss.at[h], k_rs.at[h], at(1)).start()
-        remote(v_s.at[:, columns(h)], vp.at[h], v_ss.at[h], v_rs.at[h], at(1)).start()
-        return carry
+        remote(k_s.at[:, columns(h)], kvp.at[h, 0], sent.at[0], kv_rs.at[h], at(1)).start()
+        remote(v_s.at[:, columns(h)], kvp.at[h, 1], sent.at[0], kv_rs.at[h], at(1)).start()
+        return carry
+
+    def send_back(h, carry):
+        remote(dks.at[h], dkvn.at[h, 0], sent.at[1], dkv_rs.at[h], at(-1)).start()
+        remote(dvs.at[h], dkvn.at[h, 1], sent.at[1], dkv_rs.at[h], at(-1)).start()
+        return carry
+
+    def bulk(where):
+        for h in KV_AT.get(where, ()):
+            send_kv(h, 0)
+        for h in BACK_AT.get(where, ()):
+            send_back(h, 0)
 
     loads[5].wait()
-    for h in range(4):
-        send_kv(h, 0)
+    bulk("start")
 
     def tails(h, carry):
         fx[place_of(h)] = dot_tn(fk[h], v_s[:, columns(h)]).astype(BF16)
@@ -157,9 +172,11 @@
     f_pair.start()
 
     def await_ids(near_by):
-        for i, d in enumerate(id_sends):
-            if (abs(d) == 1) == near_by:
-                remote(idr.at[REACH], idr.at[REACH - d], ids_ss.at[i], ids_rs.at[i], at(d)).wait()
+        if near_by:
+            arrival(idr.at[REACH - 1], ids_rs.at[0])
+            arrival(idr.at[REACH + 1], ids_rs.at[1])
+        else:
+            arrival(idr.at[pl.ds(0, len(id_sends) - 2)], ids_rs.at[2])
 
     await_ids(True)
 
@@ -255,6 +272,7 @@
 
     f_pair.wait_recv()
     combine(fx, fxp, ftc, fta, f_ss, f_rs, is_late + is_early * m_in, is_early + is_late * m_in)
+    bulk("f1")
     loads[6].wait()
     loads[7].wait()
     scaling = DIM ** -0.5
@@ -264,7 +282,7 @@
         q = q_s[:, columns(h)]
         k = k_s[:, columns(h)]
         v = v_s[:, columns(h)]
-        keys, values = kp[h], vp[h]
+        keys, values = kvp[h, 0], kvp[h, 1]
         ga = (g_s[:, columns(h)].astype(F32) * (1.0 - gt[h])).astype(BF16)
         s0 = dot_nt(keys, q) * scale2 + bias[0]
         s1 = dot_nt(k, q) * scale2 + bias[1]
@@ -293,32 +311,21 @@
         dvl[h] = dot_nn(wb1, ga)
         return carry
 
-    def send_back(h, carry):
-        remote(dks.at[h], dkn.at[h], dk_ss.at[h], dk_rs.at[h], at(-1)).start()
-        remote(dvs.at[h], dvn.at[h], dv_ss.at[h], dv_rs.at[h], at(-1)).start()
-        return carry
-
-    def arrived(h, carry):
-        remote(k_s.at[:, columns(h)], kp.at[h], k_ss.at[h], k_rs.at[h], at(1)).wait_recv()
-        remote(v_s.at[:, columns(h)], vp.at[h], v_ss.at[h], v_rs.at[h], at(1)).wait_recv()
-        return carry
-
-    def local_heads(low, more=()):
+    def arrived(h):
+        arrival(kvp.at[h], kv_rs.at[h])
+
+    def local_heads(low):
         for h in range(low, low + 2):
-            arrived(h, 0)
+            arrived(h)
         lax.fori_loop(low, low + 2, local, 0, unroll=UNROLL)
-        for h in range(low, low + 2):
-            send_back(h, 0)
-        for h in more:
-            send_kv(h, 0)
+        bulk(f"l{low}")
 
     await_ids(False)
     kappa, m_before = far_masks()
     told(0)
     tell(1)
 
-    for d in range(1, REACH + 1):
-        remote(zt, zr.at[d - 1], z_ss.at[d - 1], z_rs.at[d - 1], at(d)).wait_recv()
+    arrival(zr, z_rs)
     total = jnp.zeros((HEADS, 1, DIM), F32)
     for d in range(1, REACH + 1):
         weight = same(-d, -1) * (me >= d).astype(F32)
@@ -339,7 +346,7 @@
 
     for i in range(4):
         lax.fori_loop(4 * i, 4 * i + 4, state_part, 0, unroll=4)
-        send_kv(4 + i, 0)
+        bulk(f"s{i}")
     b_pair = pair_send(bx, bxp, b_ss, b_rs)
     b_pair.start()
 
@@ -347,21 +354,23 @@
         gg[h] = gg[h] + rows * (1.0 - gt[h])
 
     ring_out(fta, fro, fri, ftc, f_ss, f_rs, True)
-    local_heads(0, (8,))
+    local_heads(0)
     b_pair.wait_recv()
     combine(bx, bxp, btc, bta, b_ss, b_rs, is_early + is_late * m_before, is_late + is_early * m_before)
-    send_kv(9, 0)
-    local_heads(2, (10,))
+    bulk("b1")
+    local_heads(2)
     told(1)
     tell(2)
-    local_heads(4, (11,))
+    local_heads(4)
     spread(fta, fro, fri, fpo, fpc, f_ss, f_rs, True)
-    local_heads(6, (12, 13))
-    local_heads(8, (14, 15))
+    bulk("f2")
+    local_heads(6)
+    local_heads(8)
     ring_out(bta, bro, bri, btc, b_ss, b_rs, False)
     local_heads(10)
     local_heads(12)
     spread(bta, bro, bri, bpo, bpc, b_ss, b_rs, False)
+    bulk("b2")
     local_heads(14)
 
     for i in range(2):
@@ -387,16 +396,16 @@
 
     def x_copy(d):
         i = d - 1
-        return remote(red_s.at[0], red_r.at[i], red_ss.at[i], red_rs.at[i], at(ROW * d))
+        return remote(red_s.at[0], red_r.at[i], sent.at[5], red_rs.at[0], at(ROW * d))
 
     def z_copy(d):
         j = n_rows - 1 + d - 1
-        return remote(red_s.at[1], red_r.at[j], red_ss.at[j], red_rs.at[j], up(d))
+        return remote(red_s.at[1], red_r.at[j], sent.at[6], red_rs.at[1], up(d))
 
     def row_copy(d):
         to = {"ctx": row * ROW + lax.rem(spot + d, ROW)}
         j = n_rows - 1 + n_dp - 1 + d - 1
-        return remote(red_s.at[2], red_r.at[j], red_ss.at[j], red_rs.at[j], to)
+        return remote(red_s.at[2], red_r.at[j], sent.at[7], red_rs.at[2], to)
 
     for d in range(1, n_rows):
         x_copy(d).start()
@@ -405,8 +414,8 @@
         is_late, is_early + is_late * m_before, is_early, is_late + is_early * m_before,
     )
     told(2)
+    arrival(red_r.at[pl.ds(0, n_rows - 1)], red_rs.at[0])
     for d in range(1, n_rows):
-        x_copy(d).wait_recv()
         mine = mine + red_r[d - 1]
     red_s[1] = mine
     for d in hops:
@@ -434,7 +443,7 @@
 
     lax.fori_loop(0, HEADS, reads, 0, unroll=4)
     for d in range(1, REACH + 1):
-        remote(dzt, dzr.at[d - 1], dz_ss.at[d - 1], dz_rs.at[d - 1], at(-d)).start()
+        remote(dzt, dzr.at[d - 1], sent.at[4], dz_rs, at(-d)).start()
 
     half = HEADS * DIM // 2
 
@@ -451,8 +460,7 @@
         is_early, is_late + is_early * m_in, is_late, is_early + is_late * m_in,
     )
 
-    for d in range(1, REACH + 1):
-        remote(dzt, dzr.at[d - 1], dz_ss.at[d - 1], dz_rs.at[d - 1], at(-d)).wait_recv()
+    arrival(dzr, dz_rs)
     total = jnp.zeros((HEADS, 1, DIM), F32)
     for d in range(1, REACH + 1):
         weight = same(d - 1, 0) * (me + d < n_ctx).astype(F32)
@@ -466,14 +474,13 @@
         lifted = fk[h]
         back = dot_nt(v_s[:, columns(h)], carried) + cz[h]
         mem_key = back * jnp.minimum(lifted.astype(F32), 1.0)
-        dk_o[:, columns(h)] = (dkl[h] + dkn[h].astype(F32) + mem_key).astype(BF16)
+        dk_o[:, columns(h)] = (dkl[h] + dkvn[h, 0].astype(F32) + mem_key).astype(BF16)
         mem_value = dot_nn(lifted, carried)
-        dv_o[:, columns(h)] = (dvl[h] + dvn[h].astype(F32) + mem_value).astype(BF16)
+        dv_o[:, columns(h)] = (dvl[h] + dkvn[h, 1].astype(F32) + mem_value).astype(BF16)
         return carry
 
     def returned(h, carry):
-        remote(dks.at[h], dkn.at[h], dk_ss.at[h], dk_rs.at[h], at(-1)).wait_recv()
-        remote(dvs.at[h], dvn.at[h], dv_ss.at[h], dv_rs.at[h], at(-1)).wait_recv()
+        arrival(dkvn.at[h], dkv_rs.at[h])
         return carry
 
     for i in range(2):
@@ -482,26 +489,25 @@
         lax.fori_loop(low, high, writes, 0, unroll=4)
         put(i, 2).start()
         put(i, 3).start()
+    if hops:
+        arrival(red_r.at[pl.ds(n_rows - 1, n_dp - 1)], red_rs.at[1])
     for d in hops:
-        z_copy(d).wait_recv()
         mine = mine + red_r[n_rows - 1 + d - 1]
     red_s[2] = mine
     for d in range(1, ROW):
         row_copy(d).start()
+    arrival(red_r.at[pl.ds(n_rows + n_dp - 2, ROW - 1)], red_rs.at[2])
     for d in range(1, ROW):
-        row_copy(d).wait_recv()
         mine = mine + red_r[n_rows - 1 + n_dp - 1 + d - 1]
     gg_out[...] = mine[:, :HEADS]
 
-    for d in hops:
-        z_copy(d).wait_send()
-    for d in range(1, n_rows):
-        x_copy(d).wait_send()
-    for d in range(1, ROW):
-        row_copy(d).wait_send()
-    for d in range(1, REACH + 1):
-        remote(zt, zr.at[d - 1], z_ss.at[d - 1], z_rs.at[d - 1], at(d)).wait_send()
-        remote(dzt, dzr.at[d - 1], dz_ss.at[d - 1], dz_rs.at[d - 1], at(-d)).wait_send()
+    if hops:
+        arrival(red_r.at[pl.ds(n_rows - 1, n_dp - 1)], sent.at[6])
+    arrival(red_r.at[pl.ds(0, n_rows - 1)], sent.at[5])
+    arrival(red_r.at[pl.ds(n_rows + n_dp - 2, ROW - 1)], sent.at[7])
+    arrival(idr.at[pl.ds(0, len(id_sends))], sent.at[2])
+    arrival(zr, sent.at[3])
+    arrival(dzr, sent.at[4])
     for x, xp, tc, ta, ro, ri, po, pc, sx, res, ss, rs, forward in (
         (fx, fxp, ftc, fta, fro, fri, fpo, fpc, fsx, fres, f_ss, f_rs, True),
         (bx, bxp, btc, bta, bro, bri, bpo, bpc, bsx, bres, b_ss, b_rs, False),
@@ -513,14 +519,8 @@
         remote(ro, ri, ss.at[4], rs.at[4], at(ROW if forward else -ROW)).wait_send()
         final(sx, res, ss, rs).wait_send()
 
-    def drain(h, carry):
-        remote(k_s.at[:, columns(h)], kp.at[h], k_ss.at[h], k_rs.at[h], at(1)).wait_send()
-        remote(v_s.at[:, columns(h)], vp.at[h], v_ss.at[h], v_rs.at[h], at(1)).wait_send()
-        remote(dks.at[h], dkn.at[h], dk_ss.at[h], dk_rs.at[h], at(-1)).wait_send()
-        remote(dvs.at[h], dvn.at[h], dv_ss.at[h], dv_rs.at[h], at(-1)).wait_send()
-        return carry
-
-    lax.fori_loop(0, HEADS, drain, 0)
+    arrival(kvp, sent.at[0])
+    arrival(dkvn, sent.at[1])
     for i in range(2):
         for which in range(4):
             put(i, which).wait()
@@ -548,6 +548,7 @@
     def part(n):
         return pltpu.VMEM((n, DIM, DIM), BF16)
 
+    pair_of = pltpu.VMEM((HEADS, 2, DIM, DIM), BF16)
     lanes = pltpu.VMEM((HEADS, 1, DIM), F32)
     reach = pltpu.VMEM((REACH, HEADS, 1, DIM), F32)
     rows = pltpu.VMEM(flat, BF16)
@@ -557,17 +558,16 @@
     scratch = (
         [rows] * 4
         + [pltpu.VMEM((2 * REACH + 1, 1, DIM), jnp.int32)]
-        + [half] * 4 + [full] * 2
+        + [pair_of] + [half] * 2 + [full] * 2
         + exchange + exchange
-        + [full] * 4 + [half] * 4 + [rows] * 4
+        + [full] * 4 + [half] * 2 + [pair_of] + [rows] * 4
         + [lanes, reach, lanes, lanes, reach, lanes, lanes, lanes]
         + [pltpu.VMEM((2, SEG, SEG), F32), pltpu.VMEM((SEG, SEG), F32), pltpu.VMEM((SEG, DIM), F32)]
         + [pltpu.VMEM((3, 1, DIM), F32), pltpu.VMEM((n_red, 1, DIM), F32)]
-        + [dma((8,)), dma((8,)), pltpu.SemaphoreType.REGULAR((3,)), dma((15,)), dma((15,))]
-        + [dma((REACH,))] * 4
-        + [dma((HEADS,))] * 8
+        + [dma((8,)), dma((8,)), pltpu.SemaphoreType.REGULAR((3,)), dma((8,)), dma((3,)), dma(()), dma(())]
+        + [dma((HEADS,))] * 2
         + [dma((9,))] * 4
-        + [dma((n_red,))] * 2
+        + [dma((3,))]
     )
     shapes = [wide] * 4 + [jax.ShapeDtypeStruct((1, HEADS), F32)]
     results = pl.pallas_call(

time: 69.1 us -> 61.4 us (0.89)
  Pallas kernels: 67.6 us -> 59.9 us
    pallas_call x1, Pallas kernels: 66.3 us -> 58.5 us  [on_device(): pl.pallas_call(functools.partial(kernel, n_ctx, n_dp), out_shape=shapes,...]
where the time goes in v3:
time: 61.4 us; the launch traced here: 61.2 us
  Pallas kernels  59.9 us (98%)
  local copies, waits for them, and re-layouts  0.66 us (1%)
  between operations  0.66 us (1%)
    pallas_call x1, Pallas kernels, on_device(): pl.pallas_call(functools.partial(kernel, n_ctx, n_dp), out_shape=shapes,...  58.5 us
    pallas_call x1, Pallas kernels, on_device(): pl.pallas_call(write_out, out_shape=shapes, in_specs=[vmem] * 5, out_spec...  1.36 us

profile of v3, /device:TPU:1, one launch (start us, length us, event | category | flops | bytes accessed | tf_op | source)
XLA Modules:
  0.0 61.2 jit_solution(10253936668318455739)
XLA Ops:
  0.6 0.0 copy-start
  0.6 0.0 copy-start.1
  0.7 0.6 %copy-done = s32[1,128]{1,0:T(1,128)S(1)} copy-done((s32[1,128]{1,0:T(1,128)S(1)}, s32[1,128]{1,0:T(1,128)}, u32[]{:S(2)}) %copy-start) | copy-done | bytes 536
  1.3 0.0 copy-done.1
  1.3 58.5 %shard_map.101 = (bf16[128,2048]{1,0:T(8,128)(2,1)S(1)}, bf16[128,2048]{1,0:T(8,128)(2,1)S(1)}, bf16[128,2048]{1,0:T(8,128)(2,1)S(1)}, bf16[128,2048]{1,0:T(8,128)(2,1)S(1)}, f32[1,16]{1,0:T(1,128)S(1)}) custom-call(bf16[128,2048]{1,0:T(8,128)(2,1)} %bitcast.11, bf16[128,2048]{1,0:T(8,128)(2,1)} %bitcast.12, bf16[128,2048]{1,0:T(8,128)(2,1)} %bitcast.13, ...), custom_call_target="tpu_custom_call" | custom-call | tf_op jit(solution)/shard_map/pallas_call | solution.py:573
  59.8 1.4 %shard_map.102 = (bf16[128,2048]{1,0:T(8,128)(2,1)}, bf16[128,2048]{1,0:T(8,128)(2,1)}, bf16[128,2048]{1,0:T(8,128)(2,1)}, bf16[128,2048]{1,0:T(8,128)(2,1)}, f32[1,16]{1,0:T(1,128)}) custom-call(bf16[128,2048]{1,0:T(8,128)(2,1)S(1)} %get-tuple-element.15.refs_0_, bf16[128,2048]{1,0:T(8,128)(2,1)S(1)} %get-tuple-element.16.refs_1_, ...), custom_call_target="tpu_custom_call" | custom-call | tf_op jit(solution)/shard_map/pallas_call | solution.py:589
Async XLA Ops:
  0.6 0.7 %copy-start = (s32[1,128]{1,0:T(1,128)S(1)}, s32[1,128]{1,0:T(1,128)}, u32[]{:S(2)}) copy-start(s32[1,128]{1,0:T(1,128)} %ids_in.1) | copy-start | bytes 1540
  0.6 0.7 %copy-start.1 = (f32[16]{0:T(128)S(1)}, f32[16]{0:T(128)}, u32[]{:S(2)}) copy-start(f32[16]{0:T(128)} %param.10) | copy-start | bytes 196

commit v4 on v3

--- a/solution.py
+++ b/solution.py
@@ -14,7 +14,7 @@
 ROW = 8
 REACH = 8
 UNROLL = 2
-KV_AT = {"start": (0, 1), "f1": (2, 3, 4, 5), "s2": (6,), "b1": (7, 8, 9), "f2": (10, 11, 12), "l8": (13, 14, 15)}
+KV_AT = {"start": (0, 1), "f1": (2, 3, 4, 5), "s2": (6,), "b1": (7, 8, 9), "l2": (10,), "f2": (11, 12, 13), "l6": (14, 15)}
 BACK_AT = {f"l{h}": (h, h + 1) for h in range(0, 16, 2)}
 SCOPED = 103 * 2**19
 MESH = pl.DeviceIdType.MESH
@@ -367,6 +367,10 @@
     local_heads(6)
     local_heads(8)
     ring_out(bta, bro, bri, btc, b_ss, b_rs, False)
+    finish_start(
+        fx, fxp, fpo, fpc, fsx, fres, f_ss, f_rs,
+        is_late, is_early + is_late * m_before, is_early, is_late + is_early * m_before,
+    )
     local_heads(10)
     local_heads(12)
     spread(bta, bro, bri, bpo, bpc, b_ss, b_rs, False)
@@ -409,17 +413,7 @@
 
     for d in range(1, n_rows):
         x_copy(d).start()
-    finish_start(
-        fx, fxp, fpo, fpc, fsx, fres, f_ss, f_rs,
-        is_late, is_early + is_late * m_before, is_early, is_late + is_early * m_before,
-    )
     told(2)
-    arrival(red_r.at[pl.ds(0, n_rows - 1)], red_rs.at[0])
-    for d in range(1, n_rows):
-        mine = mine + red_r[d - 1]
-    red_s[1] = mine
-    for d in hops:
-        z_copy(d).start()
     final(fsx, fres, f_ss, f_rs, False).wait_recv()
 
     def reads(h, carry):
@@ -445,6 +439,12 @@
     for d in range(1, REACH + 1):
         remote(dzt, dzr.at[d - 1], sent.at[4], dz_rs, at(-d)).start()
 
+    arrival(red_r.at[pl.ds(0, n_rows - 1)], red_rs.at[0])
+    for d in range(1, n_rows):
+        mine = mine + red_r[d - 1]
+    red_s[1] = mine
+    for d in hops:
+        z_copy(d).start()
     half = HEADS * DIM // 2
 
     def put(i, which):

time: 61.4 us -> 61.3 us (level)
  no operation moved by 1% of the time
where the time goes in v4:
time: 61.3 us; the launch traced here: 61.2 us
  Pallas kernels  59.9 us (98%)
  local copies, waits for them, and re-layouts  0.66 us (1%)
  between operations  0.66 us (1%)
    pallas_call x1, Pallas kernels, on_device(): pl.pallas_call(functools.partial(kernel, n_ctx, n_dp), out_shape=shapes,...  58.5 us
    pallas_call x1, Pallas kernels, on_device(): pl.pallas_call(write_out, out_shape=shapes, in_specs=[vmem] * 5, out_spec...  1.36 us

profile of v4, /device:TPU:1, one launch (start us, length us, event | category | flops | bytes accessed | tf_op | source)
XLA Modules:
  0.0 61.2 jit_solution(16752710975152635695)
XLA Ops:
  0.6 0.0 copy-start
  0.6 0.0 copy-start.1
  0.7 0.6 %copy-done = s32[1,128]{1,0:T(1,128)S(1)} copy-done((s32[1,128]{1,0:T(1,128)S(1)}, s32[1,128]{1,0:T(1,128)}, u32[]{:S(2)}) %copy-start) | copy-done | bytes 536
  1.3 0.0 copy-done.1
  1.3 58.5 %shard_map.101 = (bf16[128,2048]{1,0:T(8,128)(2,1)S(1)}, bf16[128,2048]{1,0:T(8,128)(2,1)S(1)}, bf16[128,2048]{1,0:T(8,128)(2,1)S(1)}, bf16[128,2048]{1,0:T(8,128)(2,1)S(1)}, f32[1,16]{1,0:T(1,128)S(1)}) custom-call(bf16[128,2048]{1,0:T(8,128)(2,1)} %bitcast.11, bf16[128,2048]{1,0:T(8,128)(2,1)} %bitcast.12, bf16[128,2048]{1,0:T(8,128)(2,1)} %bitcast.13, ...), custom_call_target="tpu_custom_call" | custom-call | tf_op jit(solution)/shard_map/pallas_call | solution.py:573
  59.8 1.4 %shard_map.102 = (bf16[128,2048]{1,0:T(8,128)(2,1)}, bf16[128,2048]{1,0:T(8,128)(2,1)}, bf16[128,2048]{1,0:T(8,128)(2,1)}, bf16[128,2048]{1,0:T(8,128)(2,1)}, f32[1,16]{1,0:T(1,128)}) custom-call(bf16[128,2048]{1,0:T(8,128)(2,1)S(1)} %get-tuple-element.15.refs_0_, bf16[128,2048]{1,0:T(8,128)(2,1)S(1)} %get-tuple-element.16.refs_1_, ...), custom_call_target="tpu_custom_call" | custom-call | tf_op jit(solution)/shard_map/pallas_call | solution.py:589
Async XLA Ops:
  0.6 0.7 %copy-start = (s32[1,128]{1,0:T(1,128)S(1)}, s32[1,128]{1,0:T(1,128)}, u32[]{:S(2)}) copy-start(s32[1,128]{1,0:T(1,128)} %ids_in.1) | copy-start | bytes 1540
  0.6 0.7 %copy-start.1 = (f32[16]{0:T(128)S(1)}, f32[16]{0:T(128)}, u32[]{:S(2)}) copy-start(f32[16]{0:T(128)} %param.10) | copy-start | bytes 196
